TPU v7x, 512 devices: a whole 4x4x16 slice. The times are simulated.
512 devices in a mesh: seq: 32 (over y, z_lo), head: 16 (over x, z_hi, core).
Axes of the slice: x: 4, y: 4, z: 16 (z_hi: 2, z_lo: 8; z = z_hi * 8 + z_lo), core: 2. Of those that a mesh axis runs over, the one named last changes fastest.
Arguments:
- queries: bfloat16 [16384, 2048], P('seq', 'head'), may hold values from -4.5 to 4.5
- keys: bfloat16 [16384, 2048], P('seq', 'head'), may hold values from -4.5 to 4.5
- values: bfloat16 [16384, 2048], P('seq', 'head'), may hold values from -6 to 6
- grad_out: bfloat16 [16384, 2048], P('seq', 'head'), may hold values from -6 to 6
- block_perm: int32 [16, 32], P('head'), may hold values from 0 to 31, as said below
Outputs:
- attended: bfloat16 [16384, 2048], P('seq', 'head')
- grad_queries: bfloat16 [16384, 2048], P('seq', 'head')
- grad_keys: bfloat16 [16384, 2048], P('seq', 'head')
- grad_values: bfloat16 [16384, 2048], P('seq', 'head')
Inputs may be any that keep to these rules, and one draw needn't show every extreme that they name: Each row of block_perm is a permutation of 0 to 31.
All inputs are finite; a program needn't handle non-finite values.
Results may differ from a plain program's by a relative error of at most 0.007.
Values may be sent and summed in bfloat16 or wider, within the bound.
A program may use at most 64 MiB of HBM per device.

v0:
```python
import jax
import jax.numpy as jnp
from jax import lax
from jax.sharding import PartitionSpec as P

BLK = 512


def from_partner(value, axis, apart):
    mask = 2**apart
    pairs = [(source, source ^ mask) for source in range(lax.axis_size(axis))]
    return lax.ppermute(value, axis, pairs)


def passed_along(value, axis, steps):
    count = lax.axis_size(axis)
    first, last = (max(0, -steps), min(count, count - steps))
    return lax.ppermute(value, axis, [(source, source + steps) for source in range(first, last)])


def window_block(query_rows, window, grad_rows, has_prev):
    width = query_rows.shape[1]
    span = query_rows.shape[0]
    scale = width ** (-0.5)
    win_keys = window[:, :width]
    win_values = window[:, width:]
    scores = jnp.dot(query_rows, win_keys.T, preferred_element_type=jnp.float32) * scale
    column = jnp.arange(window.shape[0], dtype=jnp.int32)
    allowed = jnp.logical_or(column >= span, has_prev)
    scores = jnp.where(allowed[None, :], scores, -1e30)
    top = jnp.max(scores, axis=1, keepdims=True)
    expon = jnp.exp(scores - top)
    probs = expon / jnp.sum(expon, axis=1, keepdims=True)
    probs_low = probs.astype(jnp.bfloat16)
    attended = jnp.dot(probs_low, win_values, preferred_element_type=jnp.float32).astype(
        jnp.bfloat16
    )
    grad_probs = jnp.dot(grad_rows, win_values.T, preferred_element_type=jnp.float32)
    delta = jnp.sum(probs * grad_probs, axis=1, keepdims=True)
    grad_scores = (probs * (grad_probs - delta) * scale).astype(jnp.bfloat16)
    grad_query = jnp.dot(grad_scores, win_keys, preferred_element_type=jnp.float32).astype(
        jnp.bfloat16
    )
    grad_key = jnp.dot(grad_scores.T, query_rows, preferred_element_type=jnp.float32)
    grad_value = jnp.dot(probs_low.T, grad_rows, preferred_element_type=jnp.float32)
    window_grads = jnp.concatenate([grad_key, grad_value], axis=1).astype(jnp.bfloat16)
    return (attended, grad_query, window_grads)


def device_place(device, halvings):
    flipped = jnp.zeros_like(device)
    for bit_number in range(halvings):
        flipped = flipped + jnp.right_shift(device, bit_number) % 2 * (
            1 << halvings - 1 - bit_number
        )
    return flipped


def device_bit(bit_number, low_bits, halvings):
    offset = bit_number - low_bits
    return halvings - 1 - offset


def sort_sections(perm_row, seq_index, blocks_here, low_bits, halvings):
    block_count = perm_row.shape[0]
    element_ids = jnp.arange(block_count, dtype=jnp.int32)

    def position(block_ids):
        return block_ids % blocks_here + blocks_here * device_place(
            block_ids // blocks_here, halvings
        )

    inverse = jnp.zeros((block_count,), jnp.int32).at[perm_row].set(element_ids)
    keys_now = jnp.zeros((block_count,), jnp.int32).at[position(element_ids)].set(position(inverse))
    my_places = jnp.arange(blocks_here, dtype=jnp.int32) + blocks_here * device_place(
        seq_index, halvings
    )
    section_list = []
    for section_level in range(1, low_bits + halvings + 1):
        for bit_number in range(section_level - 1, -1, -1):
            partner_keys = jnp.take(keys_now, jnp.bitwise_xor(element_ids, 1 << bit_number))
            rising = jnp.right_shift(element_ids, section_level) % 2 == 0
            low_side = jnp.right_shift(element_ids, bit_number) % 2 == 0
            kept_keys = jnp.where(
                rising == low_side,
                jnp.minimum(keys_now, partner_keys),
                jnp.maximum(keys_now, partner_keys),
            )
            moved_flags = kept_keys != keys_now
            section_list.append((bit_number, jnp.take(moved_flags, my_places)))
            keys_now = kept_keys
    return section_list


def route_blocks(blocks, section_list, low_bits, halvings, returning):
    ordered = list(reversed(section_list)) if returning else section_list
    for bit_number, moved_flags in ordered:
        if returning:
            partner_blocks = from_partner(blocks, "seq", device_bit(bit_number, low_bits, halvings))
        else:
            partner_blocks = from_partner(blocks, "seq", device_bit(bit_number, low_bits, halvings))
        blocks = jnp.where(moved_flags[:, None, None], partner_blocks, blocks)
    return blocks


def body(queries, keys, values, grad_out, block_perm):
    width = queries.shape[1]
    blocks_here = queries.shape[0] // BLK
    halvings = lax.axis_size("seq").bit_length() - 1
    low_bits = blocks_here.bit_length() - 1
    seq_index = lax.axis_index("seq")
    query_blocks = queries.reshape(blocks_here, BLK, width)
    grad_blocks = grad_out.reshape(blocks_here, BLK, width)
    pair = jnp.concatenate(
        [keys.reshape(blocks_here, BLK, width), values.reshape(blocks_here, BLK, width)], axis=2
    )
    section_list = sort_sections(block_perm[0], seq_index, blocks_here, low_bits, halvings)
    slot_ids = jnp.arange(blocks_here, dtype=jnp.int32)
    prev_pair = passed_along(pair[blocks_here - 1], "seq", 1)
    far_pair = route_blocks(pair, section_list, low_bits, halvings, False)
    previous = jnp.concatenate([prev_pair[None], pair[:-1]], axis=0)
    windows = jnp.concatenate([previous, pair, far_pair], axis=1)
    has_prev = seq_index * blocks_here + slot_ids > 0

    def one_block(items):
        return window_block(items[0], items[1], items[2], items[3])

    attended, grad_query, window_grads = lax.map(
        one_block, (query_blocks, windows, grad_blocks, has_prev)
    )
    far_back = route_blocks(window_grads[:, 2 * BLK :], section_list, low_bits, halvings, True)
    prev_back = passed_along(window_grads[0, :BLK], "seq", -1)
    local_part = window_grads[:, BLK : 2 * BLK].astype(jnp.float32)
    prev_moved = jnp.concatenate([window_grads[1:, :BLK], prev_back[None]], axis=0).astype(
        jnp.float32
    )
    far_moved = far_back.astype(jnp.float32)
    total = (
        (local_part + prev_moved + far_moved)
        .astype(jnp.bfloat16)
        .reshape(blocks_here * BLK, 2 * width)
    )
    return (
        attended.reshape(blocks_here * BLK, width),
        grad_query.reshape(blocks_here * BLK, width),
        total[:, :width],
        total[:, width:],
    )


def solution(mesh):
    placed = (
        P("seq", "head"),
        P("seq", "head"),
        P("seq", "head"),
        P("seq", "head"),
        P("head", None),
    )
    return jax.shard_map(
        body,
        mesh=mesh,
        in_specs=placed,
        out_specs=(P("seq", "head"), P("seq", "head"), P("seq", "head"), P("seq", "head")),
        check_vma=False,
    )
```

profile of v0, /device:TPU:6, one launch (start us, length us, event | category | flops | bytes accessed | tf_op | source)
XLA Modules:
  0.0 422.6 jit_solution(1495473761233881073)
XLA Ops:
  2.7 5.1 %collective-permute-start.1 = (bf16[1,512,256]{1,2,0:T(8,128)(2,1)S(1)}, bf16[1,512,256]{1,2,0:T(8,128)(2,1)S(1)}, u32[]{:S(2)}, u32[]{:S(2)}) collective-permute-start(bf16[1,512,256]{1,2,0:T(8,128)(2,1)S(1)} %pad_maximum_fusion.1), channel_id=1, source_target_pairs={{0,256},{16,272},{32,288},{48,304},{64,320},{80,336},{96,352},{112... | collective-permute-start | bytes 786440 | tf_op jit(solution)/shard_map/ppermute | solution.py:12
  12.0 2.2 collective-permute-done.1
  14.3 3.5 collective-permute-start.2
  20.4 2.9 collective-permute-done.2
  23.4 5.1 %collective-permute-start.3 = (bf16[1,512,256]{1,2,0:T(8,128)(2,1)S(1)}, bf16[1,512,256]{1,2,0:T(8,128)(2,1)S(1)}, u32[]{:S(2)}, u32[]{:S(2)}) collective-permute-start(bf16[1,512,256]{1,2,0:T(8,128)(2,1)S(1)} %broadcast_select_fusion.2), channel_id=1, source_target_pairs={{0,256},{16,272},{32,288},{48,304},{64,320},{80,336},{96,352},{112... | collective-permute-start | bytes 786440 | tf_op jit(solution)/shard_map/ppermute | solution.py:12
  29.8 3.4 collective-permute-done.3
  33.2 9.1 %collective-permute-start.4 = (bf16[1,512,256]{1,2,0:T(8,128)(2,1)S(1)}, bf16[1,512,256]{1,2,0:T(8,128)(2,1)S(1)}, u32[]{:S(2)}, u32[]{:S(2)}) collective-permute-start(bf16[1,512,256]{1,2,0:T(8,128)(2,1)S(1)} %broadcast_select_fusion.4), channel_id=1, source_target_pairs={{0,64},{16,80},{32,96},{48,112},{64,0},{80,16},{96,32},{112,48},{1... | collective-permute-start | bytes 786440 | tf_op jit(solution)/shard_map/ppermute | solution.py:12
  44.3 18.3 %collective-permute-done.4 = bf16[1,512,256]{1,2,0:T(8,128)(2,1)S(1)} collective-permute-done((bf16[1,512,256]{1,2,0:T(8,128)(2,1)S(1)}, bf16[1,512,256]{1,2,0:T(8,128)(2,1)S(1)}, u32[]{:S(2)}, u32[]{:S(2)}) %collective-permute-start.4) | collective-permute-done | bytes 262176 | tf_op jit(solution)/shard_map/ppermute | solution.py:12
  62.6 3.5 collective-permute-start.5
  68.8 2.6 collective-permute-done.5
  71.4 5.1 %collective-permute-start.6 = (bf16[1,512,256]{1,2,0:T(8,128)(2,1)S(1)}, bf16[1,512,256]{1,2,0:T(8,128)(2,1)S(1)}, u32[]{:S(2)}, u32[]{:S(2)}) collective-permute-start(bf16[1,512,256]{1,2,0:T(8,128)(2,1)S(1)} %broadcast_select_fusion.8), channel_id=1, source_target_pairs={{0,256},{16,272},{32,288},{48,304},{64,320},{80,336},{96,352},{112... | collective-permute-start | bytes 786440 | tf_op jit(solution)/shard_map/ppermute | solution.py:12
  77.7 3.4 collective-permute-done.6
  81.2 1.9 collective-permute-start.7
  85.1 13.2 %collective-permute-done.7 = bf16[1,512,256]{1,2,0:T(8,128)(2,1)S(1)} collective-permute-done((bf16[1,512,256]{1,2,0:T(8,128)(2,1)S(1)}, bf16[1,512,256]{1,2,0:T(8,128)(2,1)S(1)}, u32[]{:S(2)}, u32[]{:S(2)}) %collective-permute-start.7) | collective-permute-done | bytes 262176 | tf_op jit(solution)/shard_map/ppermute | solution.py:12
  98.4 1.9 collective-permute-start.8
  102.3 16.0 %collective-permute-done.8 = bf16[1,512,256]{1,2,0:T(8,128)(2,1)S(1)} collective-permute-done((bf16[1,512,256]{1,2,0:T(8,128)(2,1)S(1)}, bf16[1,512,256]{1,2,0:T(8,128)(2,1)S(1)}, u32[]{:S(2)}, u32[]{:S(2)}) %collective-permute-start.8) | collective-permute-done | bytes 262176 | tf_op jit(solution)/shard_map/ppermute | solution.py:12
  118.3 3.5 collective-permute-start.9
  124.5 2.0 collective-permute-done.9
  126.6 5.1 %collective-permute-start.10 = (bf16[1,512,256]{1,2,0:T(8,128)(2,1)S(1)}, bf16[1,512,256]{1,2,0:T(8,128)(2,1)S(1)}, u32[]{:S(2)}, u32[]{:S(2)}) collective-permute-start(bf16[1,512,256]{1,2,0:T(8,128)(2,1)S(1)} %broadcast_select_fusion.16), channel_id=1, source_target_pairs={{0,256},{16,272},{32,288},{48,304},{64,320},{80,336},{96,352},{112... | collective-permute-start | bytes 786440 | tf_op jit(solution)/shard_map/ppermute | solution.py:12
  132.8 3.5 collective-permute-done.10
  136.4 1.9 collective-permute-start.11
  140.3 4.3 %collective-permute-done.11 = bf16[1,512,256]{1,2,0:T(8,128)(2,1)S(1)} collective-permute-done((bf16[1,512,256]{1,2,0:T(8,128)(2,1)S(1)}, bf16[1,512,256]{1,2,0:T(8,128)(2,1)S(1)}, u32[]{:S(2)}, u32[]{:S(2)}) %collective-permute-start.11) | collective-permute-done | bytes 262176 | tf_op jit(solution)/shard_map/ppermute | solution.py:12
  144.7 3.9 collective-permute-start.12
  150.4 8.0 %collective-permute-done.12 = bf16[1,512,256]{1,2,0:T(8,128)(2,1)S(1)} collective-permute-done((bf16[1,512,256]{1,2,0:T(8,128)(2,1)S(1)}, bf16[1,512,256]{1,2,0:T(8,128)(2,1)S(1)}, u32[]{:S(2)}, u32[]{:S(2)}) %collective-permute-start.12) | collective-permute-done | bytes 262176 | tf_op jit(solution)/shard_map/ppermute | solution.py:12
  158.4 8.4 %collective-permute-start.13 = (bf16[1,512,256]{1,2,0:T(8,128)(2,1)S(1)}, bf16[1,512,256]{1,2,0:T(8,128)(2,1)S(1)}, u32[]{:S(2)}, u32[]{:S(2)}) collective-permute-start(bf16[1,512,256]{1,2,0:T(8,128)(2,1)S(1)} %broadcast_select_fusion.22), channel_id=1, source_target_pairs={{0,64},{16,80},{32,96},{48,112},{64,0},{80,16},{96,32},{112,48},{1... | collective-permute-start | bytes 786440 | tf_op jit(solution)/shard_map/ppermute | solution.py:12
  168.8 19.4 %collective-permute-done.13 = bf16[1,512,256]{1,2,0:T(8,128)(2,1)S(1)} collective-permute-done((bf16[1,512,256]{1,2,0:T(8,128)(2,1)S(1)}, bf16[1,512,256]{1,2,0:T(8,128)(2,1)S(1)}, u32[]{:S(2)}, u32[]{:S(2)}) %collective-permute-start.13) | collective-permute-done | bytes 262176 | tf_op jit(solution)/shard_map/ppermute | solution.py:12
  188.3 3.5 collective-permute-start.14
  194.5 3.9 collective-permute-done.14
  198.4 5.1 %collective-permute-start.15 = (bf16[1,512,256]{1,2,0:T(8,128)(2,1)S(1)}, bf16[1,512,256]{1,2,0:T(8,128)(2,1)S(1)}, u32[]{:S(2)}, u32[]{:S(2)}) collective-permute-start(bf16[1,512,256]{1,2,0:T(8,128)(2,1)S(1)} %broadcast_select_fusion.26), channel_id=1, source_target_pairs={{0,256},{16,272},{32,288},{48,304},{64,320},{80,336},{96,352},{112... | collective-permute-start | bytes 786440 | tf_op jit(solution)/shard_map/ppermute | solution.py:12
  203.5 1.3 collective-permute-start
  206.1 3.1 collective-permute-done.15
  209.8 1.3 fusion.82
  214.7 12.6 %collective-permute-start.17 = (bf16[1,512,256]{1,2,0:T(8,128)(2,1)S(1)}, bf16[1,512,256]{1,2,0:T(8,128)(2,1)S(1)}, u32[]{:S(2)}, u32[]{:S(2)}) collective-permute-start(bf16[1,512,256]{1,2,0:T(8,128)(2,1)S(1)} %get-tuple-element.230), channel_id=1, source_target_pairs={{0,256},{16,272},{32,288},{48,304},{64,320},{80,336},{96,352},{112... | collective-permute-start | bytes 786440 | tf_op jit(solution)/shard_map/ppermute | solution.py:12
  227.2 4.5 %collective-permute-done.17 = bf16[1,512,256]{1,2,0:T(8,128)(2,1)S(1)} collective-permute-done((bf16[1,512,256]{1,2,0:T(8,128)(2,1)S(1)}, bf16[1,512,256]{1,2,0:T(8,128)(2,1)S(1)}, u32[]{:S(2)}, u32[]{:S(2)}) %collective-permute-start.17) | collective-permute-done | bytes 262176 | tf_op jit(solution)/shard_map/ppermute | solution.py:12
  231.8 5.6 %collective-permute-start.18 = (bf16[1,512,256]{1,2,0:T(8,128)(2,1)S(1)}, bf16[1,512,256]{1,2,0:T(8,128)(2,1)S(1)}, u32[]{:S(2)}, u32[]{:S(2)}) collective-permute-start(bf16[1,512,256]{1,2,0:T(8,128)(2,1)S(1)} %broadcast_select_fusion.27), channel_id=1, source_target_pairs={{0,128},{16,144},{32,160},{48,176},{64,192},{80,208},{96,224},{112... | collective-permute-start | bytes 786440 | tf_op jit(solution)/shard_map/ppermute | solution.py:12
  237.4 4.3 %collective-permute-done.18 = bf16[1,512,256]{1,2,0:T(8,128)(2,1)S(1)} collective-permute-done((bf16[1,512,256]{1,2,0:T(8,128)(2,1)S(1)}, bf16[1,512,256]{1,2,0:T(8,128)(2,1)S(1)}, u32[]{:S(2)}, u32[]{:S(2)}) %collective-permute-start.18) | collective-permute-done | bytes 262176 | tf_op jit(solution)/shard_map/ppermute | solution.py:12
  241.8 1.9 collective-permute-start.19
  243.7 17.5 %collective-permute-done.19 = bf16[1,512,256]{1,2,0:T(8,128)(2,1)S(1)} collective-permute-done((bf16[1,512,256]{1,2,0:T(8,128)(2,1)S(1)}, bf16[1,512,256]{1,2,0:T(8,128)(2,1)S(1)}, u32[]{:S(2)}, u32[]{:S(2)}) %collective-permute-start.19) | collective-permute-done | bytes 262176 | tf_op jit(solution)/shard_map/ppermute | solution.py:12
  261.2 1.9 collective-permute-start.20
  263.1 10.0 %collective-permute-done.20 = bf16[1,512,256]{1,2,0:T(8,128)(2,1)S(1)} collective-permute-done((bf16[1,512,256]{1,2,0:T(8,128)(2,1)S(1)}, bf16[1,512,256]{1,2,0:T(8,128)(2,1)S(1)}, u32[]{:S(2)}, u32[]{:S(2)}) %collective-permute-start.20) | collective-permute-done | bytes 262176 | tf_op jit(solution)/shard_map/ppermute | solution.py:12
  273.2 1.9 collective-permute-start.21
  275.1 8.2 %collective-permute-done.21 = bf16[1,512,256]{1,2,0:T(8,128)(2,1)S(1)} collective-permute-done((bf16[1,512,256]{1,2,0:T(8,128)(2,1)S(1)}, bf16[1,512,256]{1,2,0:T(8,128)(2,1)S(1)}, u32[]{:S(2)}, u32[]{:S(2)}) %collective-permute-start.21) | collective-permute-done | bytes 262176 | tf_op jit(solution)/shard_map/ppermute | solution.py:12
  283.3 2.7 collective-permute-start.22
  286.0 8.1 %collective-permute-done.22 = bf16[1,512,256]{1,2,0:T(8,128)(2,1)S(1)} collective-permute-done((bf16[1,512,256]{1,2,0:T(8,128)(2,1)S(1)}, bf16[1,512,256]{1,2,0:T(8,128)(2,1)S(1)}, u32[]{:S(2)}, u32[]{:S(2)}) %collective-permute-start.22) | collective-permute-done | bytes 262176 | tf_op jit(solution)/shard_map/ppermute | solution.py:12
  294.1 2.6 collective-permute-start.23
  296.7 5.8 %collective-permute-done.23 = bf16[1,512,256]{1,2,0:T(8,128)(2,1)S(1)} collective-permute-done((bf16[1,512,256]{1,2,0:T(8,128)(2,1)S(1)}, bf16[1,512,256]{1,2,0:T(8,128)(2,1)S(1)}, u32[]{:S(2)}, u32[]{:S(2)}) %collective-permute-start.23) | collective-permute-done | bytes 262176 | tf_op jit(solution)/shard_map/ppermute | solution.py:12
  302.6 4.3 %collective-permute-start.24 = (bf16[1,512,256]{1,2,0:T(8,128)(2,1)S(1)}, bf16[1,512,256]{1,2,0:T(8,128)(2,1)S(1)}, u32[]{:S(2)}, u32[]{:S(2)}) collective-permute-start(bf16[1,512,256]{1,2,0:T(8,128)(2,1)S(1)} %broadcast_select_fusion.15), channel_id=1, source_target_pairs={{0,64},{16,80},{32,96},{48,112},{64,0},{80,16},{96,32},{112,48},{1... | collective-permute-start | bytes 786440 | tf_op jit(solution)/shard_map/ppermute | solution.py:12
  306.9 22.9 %collective-permute-done.24 = bf16[1,512,256]{1,2,0:T(8,128)(2,1)S(1)} collective-permute-done((bf16[1,512,256]{1,2,0:T(8,128)(2,1)S(1)}, bf16[1,512,256]{1,2,0:T(8,128)(2,1)S(1)}, u32[]{:S(2)}, u32[]{:S(2)}) %collective-permute-start.24) | collective-permute-done | bytes 262176 | tf_op jit(solution)/shard_map/ppermute | solution.py:12
  329.8 1.9 collective-permute-start.25
  331.8 10.7 %collective-permute-done.25 = bf16[1,512,256]{1,2,0:T(8,128)(2,1)S(1)} collective-permute-done((bf16[1,512,256]{1,2,0:T(8,128)(2,1)S(1)}, bf16[1,512,256]{1,2,0:T(8,128)(2,1)S(1)}, u32[]{:S(2)}, u32[]{:S(2)}) %collective-permute-start.25) | collective-permute-done | bytes 262176 | tf_op jit(solution)/shard_map/ppermute | solution.py:12
  342.5 2.7 collective-permute-start.26
  345.2 8.9 %collective-permute-done.26 = bf16[1,512,256]{1,2,0:T(8,128)(2,1)S(1)} collective-permute-done((bf16[1,512,256]{1,2,0:T(8,128)(2,1)S(1)}, bf16[1,512,256]{1,2,0:T(8,128)(2,1)S(1)}, u32[]{:S(2)}, u32[]{:S(2)}) %collective-permute-start.26) | collective-permute-done | bytes 262176 | tf_op jit(solution)/shard_map/ppermute | solution.py:12
  354.1 2.6 collective-permute-start.27
  356.7 6.7 %collective-permute-done.27 = bf16[1,512,256]{1,2,0:T(8,128)(2,1)S(1)} collective-permute-done((bf16[1,512,256]{1,2,0:T(8,128)(2,1)S(1)}, bf16[1,512,256]{1,2,0:T(8,128)(2,1)S(1)}, u32[]{:S(2)}, u32[]{:S(2)}) %collective-permute-start.27) | collective-permute-done | bytes 262176 | tf_op jit(solution)/shard_map/ppermute | solution.py:12
  363.4 3.8 collective-permute-start.28
  367.2 22.1 %collective-permute-done.28 = bf16[1,512,256]{1,2,0:T(8,128)(2,1)S(1)} collective-permute-done((bf16[1,512,256]{1,2,0:T(8,128)(2,1)S(1)}, bf16[1,512,256]{1,2,0:T(8,128)(2,1)S(1)}, u32[]{:S(2)}, u32[]{:S(2)}) %collective-permute-start.28) | collective-permute-done | bytes 262176 | tf_op jit(solution)/shard_map/ppermute | solution.py:12
  389.3 2.7 collective-permute-start.29
  392.0 8.9 %collective-permute-done.29 = bf16[1,512,256]{1,2,0:T(8,128)(2,1)S(1)} collective-permute-done((bf16[1,512,256]{1,2,0:T(8,128)(2,1)S(1)}, bf16[1,512,256]{1,2,0:T(8,128)(2,1)S(1)}, u32[]{:S(2)}, u32[]{:S(2)}) %collective-permute-start.29) | collective-permute-done | bytes 262176 | tf_op jit(solution)/shard_map/ppermute | solution.py:12
  401.0 2.6 collective-permute-start.30
  403.6 1.3 convolution_convert_fusion.3
  404.9 1.3 collective-permute-start.16
  406.2 4.0 collective-permute-done.30
  410.3 5.6 %collective-permute-start.31 = (bf16[1,512,256]{1,2,0:T(8,128)(2,1)S(1)}, bf16[1,512,256]{1,2,0:T(8,128)(2,1)S(1)}, u32[]{:S(2)}, u32[]{:S(2)}) collective-permute-start(bf16[1,512,256]{1,2,0:T(8,128)(2,1)S(1)} %broadcast_select_fusion.1), channel_id=1, source_target_pairs={{0,256},{16,272},{32,288},{48,304},{64,320},{80,336},{96,352},{112... | collective-permute-start | bytes 786440 | tf_op jit(solution)/shard_map/ppermute | solution.py:12
  417.1 3.8 collective-permute-done.31
  (112 shorter events, 32.0 us)
Async XLA Ops:
  0.6 211.0 %copy-start = (bf16[512,128]{1,0:T(8,128)(2,1)S(1)}, bf16[512,128]{1,0:T(8,128)(2,1)}, u32[]{:S(2)}) copy-start(bf16[512,128]{1,0:T(8,128)(2,1)} %param.10) | copy-start | bytes 393220
  2.7 11.4 %collective-permute-start.1 = (bf16[1,512,256]{1,2,0:T(8,128)(2,1)S(1)}, bf16[1,512,256]{1,2,0:T(8,128)(2,1)S(1)}, u32[]{:S(2)}, u32[]{:S(2)}) collective-permute-start(bf16[1,512,256]{1,2,0:T(8,128)(2,1)S(1)} %pad_maximum_fusion.1), channel_id=1, source_target_pairs={{0,256},{16,272},{32,288},{48,304},{64,320},{80,336},{96,352},{112... | collective-permute-start | bytes 786440 | tf_op jit(solution)/shard_map/ppermute | solution.py:12
  14.3 9.1 %collective-permute-start.2 = (bf16[1,512,256]{1,2,0:T(8,128)(2,1)S(1)}, bf16[1,512,256]{1,2,0:T(8,128)(2,1)S(1)}, u32[]{:S(2)}, u32[]{:S(2)}) collective-permute-start(bf16[1,512,256]{1,2,0:T(8,128)(2,1)S(1)} %get-tuple-element.235), channel_id=1, source_target_pairs={{0,128},{16,144},{32,160},{48,176},{64,192},{80,208},{96,224},{112... | collective-permute-start | bytes 786440 | tf_op jit(solution)/shard_map/ppermute | solution.py:12
  23.4 9.8 %collective-permute-start.3 = (bf16[1,512,256]{1,2,0:T(8,128)(2,1)S(1)}, bf16[1,512,256]{1,2,0:T(8,128)(2,1)S(1)}, u32[]{:S(2)}, u32[]{:S(2)}) collective-permute-start(bf16[1,512,256]{1,2,0:T(8,128)(2,1)S(1)} %broadcast_select_fusion.2), channel_id=1, source_target_pairs={{0,256},{16,272},{32,288},{48,304},{64,320},{80,336},{96,352},{112... | collective-permute-start | bytes 786440 | tf_op jit(solution)/shard_map/ppermute | solution.py:12
  33.2 29.4 %collective-permute-start.4 = (bf16[1,512,256]{1,2,0:T(8,128)(2,1)S(1)}, bf16[1,512,256]{1,2,0:T(8,128)(2,1)S(1)}, u32[]{:S(2)}, u32[]{:S(2)}) collective-permute-start(bf16[1,512,256]{1,2,0:T(8,128)(2,1)S(1)} %broadcast_select_fusion.4), channel_id=1, source_target_pairs={{0,64},{16,80},{32,96},{48,112},{64,0},{80,16},{96,32},{112,48},{1... | collective-permute-start | bytes 786440 | tf_op jit(solution)/shard_map/ppermute | solution.py:12
  62.6 8.8 %collective-permute-start.5 = (bf16[1,512,256]{1,2,0:T(8,128)(2,1)S(1)}, bf16[1,512,256]{1,2,0:T(8,128)(2,1)S(1)}, u32[]{:S(2)}, u32[]{:S(2)}) collective-permute-start(bf16[1,512,256]{1,2,0:T(8,128)(2,1)S(1)} %broadcast_select_fusion.6), channel_id=1, source_target_pairs={{0,128},{16,144},{32,160},{48,176},{64,192},{80,208},{96,224},{112... | collective-permute-start | bytes 786440 | tf_op jit(solution)/shard_map/ppermute | solution.py:12
  71.4 9.8 %collective-permute-start.6 = (bf16[1,512,256]{1,2,0:T(8,128)(2,1)S(1)}, bf16[1,512,256]{1,2,0:T(8,128)(2,1)S(1)}, u32[]{:S(2)}, u32[]{:S(2)}) collective-permute-start(bf16[1,512,256]{1,2,0:T(8,128)(2,1)S(1)} %broadcast_select_fusion.8), channel_id=1, source_target_pairs={{0,256},{16,272},{32,288},{48,304},{64,320},{80,336},{96,352},{112... | collective-permute-start | bytes 786440 | tf_op jit(solution)/shard_map/ppermute | solution.py:12
  81.2 17.2 %collective-permute-start.7 = (bf16[1,512,256]{1,2,0:T(8,128)(2,1)S(1)}, bf16[1,512,256]{1,2,0:T(8,128)(2,1)S(1)}, u32[]{:S(2)}, u32[]{:S(2)}) collective-permute-start(bf16[1,512,256]{1,2,0:T(8,128)(2,1)S(1)} %broadcast_select_fusion.10), channel_id=1, source_target_pairs={{0,32},{16,48},{32,0},{48,16},{64,96},{80,112},{96,64},{112,80},{1... | collective-permute-start | bytes 786440 | tf_op jit(solution)/shard_map/ppermute | solution.py:12
  98.4 19.8 %collective-permute-start.8 = (bf16[1,512,256]{1,2,0:T(8,128)(2,1)S(1)}, bf16[1,512,256]{1,2,0:T(8,128)(2,1)S(1)}, u32[]{:S(2)}, u32[]{:S(2)}) collective-permute-start(bf16[1,512,256]{1,2,0:T(8,128)(2,1)S(1)} %broadcast_select_fusion.12), channel_id=1, source_target_pairs={{0,64},{16,80},{32,96},{48,112},{64,0},{80,16},{96,32},{112,48},{1... | collective-permute-start | bytes 786440 | tf_op jit(solution)/shard_map/ppermute | solution.py:12
  118.3 8.3 %collective-permute-start.9 = (bf16[1,512,256]{1,2,0:T(8,128)(2,1)S(1)}, bf16[1,512,256]{1,2,0:T(8,128)(2,1)S(1)}, u32[]{:S(2)}, u32[]{:S(2)}) collective-permute-start(bf16[1,512,256]{1,2,0:T(8,128)(2,1)S(1)} %broadcast_select_fusion.14), channel_id=1, source_target_pairs={{0,128},{16,144},{32,160},{48,176},{64,192},{80,208},{96,224},{112... | collective-permute-start | bytes 786440 | tf_op jit(solution)/shard_map/ppermute | solution.py:12
  126.6 9.8 %collective-permute-start.10 = (bf16[1,512,256]{1,2,0:T(8,128)(2,1)S(1)}, bf16[1,512,256]{1,2,0:T(8,128)(2,1)S(1)}, u32[]{:S(2)}, u32[]{:S(2)}) collective-permute-start(bf16[1,512,256]{1,2,0:T(8,128)(2,1)S(1)} %broadcast_select_fusion.16), channel_id=1, source_target_pairs={{0,256},{16,272},{32,288},{48,304},{64,320},{80,336},{96,352},{112... | collective-permute-start | bytes 786440 | tf_op jit(solution)/shard_map/ppermute | solution.py:12
  136.4 8.3 %collective-permute-start.11 = (bf16[1,512,256]{1,2,0:T(8,128)(2,1)S(1)}, bf16[1,512,256]{1,2,0:T(8,128)(2,1)S(1)}, u32[]{:S(2)}, u32[]{:S(2)}) collective-permute-start(bf16[1,512,256]{1,2,0:T(8,128)(2,1)S(1)} %broadcast_select_fusion.18), channel_id=1, source_target_pairs={{0,16},{16,0},{32,48},{48,32},{64,80},{80,64},{96,112},{112,96},{1... | collective-permute-start | bytes 786440 | tf_op jit(solution)/shard_map/ppermute | solution.py:12
  144.7 13.7 %collective-permute-start.12 = (bf16[1,512,256]{1,2,0:T(8,128)(2,1)S(1)}, bf16[1,512,256]{1,2,0:T(8,128)(2,1)S(1)}, u32[]{:S(2)}, u32[]{:S(2)}) collective-permute-start(bf16[1,512,256]{1,2,0:T(8,128)(2,1)S(1)} %broadcast_select_fusion.20), channel_id=1, source_target_pairs={{0,32},{16,48},{32,0},{48,16},{64,96},{80,112},{96,64},{112,80},{1... | collective-permute-start | bytes 786440 | tf_op jit(solution)/shard_map/ppermute | solution.py:12
  158.3 51.4 %copy-start.1 = (bf16[512,128]{1,0:T(8,128)(2,1)S(1)}, bf16[512,128]{1,0:T(8,128)(2,1)}, u32[]{:S(2)}) copy-start(bf16[512,128]{1,0:T(8,128)(2,1)} %param.7) | copy-start | bytes 393220
  158.4 29.8 %collective-permute-start.13 = (bf16[1,512,256]{1,2,0:T(8,128)(2,1)S(1)}, bf16[1,512,256]{1,2,0:T(8,128)(2,1)S(1)}, u32[]{:S(2)}, u32[]{:S(2)}) collective-permute-start(bf16[1,512,256]{1,2,0:T(8,128)(2,1)S(1)} %broadcast_select_fusion.22), channel_id=1, source_target_pairs={{0,64},{16,80},{32,96},{48,112},{64,0},{80,16},{96,32},{112,48},{1... | collective-permute-start | bytes 786440 | tf_op jit(solution)/shard_map/ppermute | solution.py:12
  188.3 10.1 %collective-permute-start.14 = (bf16[1,512,256]{1,2,0:T(8,128)(2,1)S(1)}, bf16[1,512,256]{1,2,0:T(8,128)(2,1)S(1)}, u32[]{:S(2)}, u32[]{:S(2)}) collective-permute-start(bf16[1,512,256]{1,2,0:T(8,128)(2,1)S(1)} %broadcast_select_fusion.24), channel_id=1, source_target_pairs={{0,128},{16,144},{32,160},{48,176},{64,192},{80,208},{96,224},{112... | collective-permute-start | bytes 786440 | tf_op jit(solution)/shard_map/ppermute | solution.py:12
  198.4 10.8 %collective-permute-start.15 = (bf16[1,512,256]{1,2,0:T(8,128)(2,1)S(1)}, bf16[1,512,256]{1,2,0:T(8,128)(2,1)S(1)}, u32[]{:S(2)}, u32[]{:S(2)}) collective-permute-start(bf16[1,512,256]{1,2,0:T(8,128)(2,1)S(1)} %broadcast_select_fusion.26), channel_id=1, source_target_pairs={{0,256},{16,272},{32,288},{48,304},{64,320},{80,336},{96,352},{112... | collective-permute-start | bytes 786440 | tf_op jit(solution)/shard_map/ppermute | solution.py:12
  203.5 6.2 %collective-permute-start = (bf16[512,256]{0,1:T(8,128)(2,1)S(1)}, bf16[512,256]{0,1:T(8,128)(2,1)S(1)}, u32[]{:S(2)}, u32[]{:S(2)}) collective-permute-start(bf16[512,256]{0,1:T(8,128)(2,1)S(1)} %get-tuple-element.234), channel_id=1, source_target_pairs={{0,16},{16,32},{32,48},{48,64},{64,80},{80,96},{96,112},{112,128},... | collective-permute-start | bytes 786440 | tf_op jit(solution)/shard_map/ppermute | solution.py:18
  214.7 17.1 %collective-permute-start.17 = (bf16[1,512,256]{1,2,0:T(8,128)(2,1)S(1)}, bf16[1,512,256]{1,2,0:T(8,128)(2,1)S(1)}, u32[]{:S(2)}, u32[]{:S(2)}) collective-permute-start(bf16[1,512,256]{1,2,0:T(8,128)(2,1)S(1)} %get-tuple-element.230), channel_id=1, source_target_pairs={{0,256},{16,272},{32,288},{48,304},{64,320},{80,336},{96,352},{112... | collective-permute-start | bytes 786440 | tf_op jit(solution)/shard_map/ppermute | solution.py:12
  231.8 10.0 %collective-permute-start.18 = (bf16[1,512,256]{1,2,0:T(8,128)(2,1)S(1)}, bf16[1,512,256]{1,2,0:T(8,128)(2,1)S(1)}, u32[]{:S(2)}, u32[]{:S(2)}) collective-permute-start(bf16[1,512,256]{1,2,0:T(8,128)(2,1)S(1)} %broadcast_select_fusion.27), channel_id=1, source_target_pairs={{0,128},{16,144},{32,160},{48,176},{64,192},{80,208},{96,224},{112... | collective-permute-start | bytes 786440 | tf_op jit(solution)/shard_map/ppermute | solution.py:12
  241.8 19.4 %collective-permute-start.19 = (bf16[1,512,256]{1,2,0:T(8,128)(2,1)S(1)}, bf16[1,512,256]{1,2,0:T(8,128)(2,1)S(1)}, u32[]{:S(2)}, u32[]{:S(2)}) collective-permute-start(bf16[1,512,256]{1,2,0:T(8,128)(2,1)S(1)} %broadcast_select_fusion.25), channel_id=1, source_target_pairs={{0,64},{16,80},{32,96},{48,112},{64,0},{80,16},{96,32},{112,48},{1... | collective-permute-start | bytes 786440 | tf_op jit(solution)/shard_map/ppermute | solution.py:12
  261.2 11.9 %collective-permute-start.20 = (bf16[1,512,256]{1,2,0:T(8,128)(2,1)S(1)}, bf16[1,512,256]{1,2,0:T(8,128)(2,1)S(1)}, u32[]{:S(2)}, u32[]{:S(2)}) collective-permute-start(bf16[1,512,256]{1,2,0:T(8,128)(2,1)S(1)} %broadcast_select_fusion.23), channel_id=1, source_target_pairs={{0,32},{16,48},{32,0},{48,16},{64,96},{80,112},{96,64},{112,80},{1... | collective-permute-start | bytes 786440 | tf_op jit(solution)/shard_map/ppermute | solution.py:12
  273.2 10.1 %collective-permute-start.21 = (bf16[1,512,256]{1,2,0:T(8,128)(2,1)S(1)}, bf16[1,512,256]{1,2,0:T(8,128)(2,1)S(1)}, u32[]{:S(2)}, u32[]{:S(2)}) collective-permute-start(bf16[1,512,256]{1,2,0:T(8,128)(2,1)S(1)} %broadcast_select_fusion.21), channel_id=1, source_target_pairs={{0,16},{16,0},{32,48},{48,32},{64,80},{80,64},{96,112},{112,96},{1... | collective-permute-start | bytes 786440 | tf_op jit(solution)/shard_map/ppermute | solution.py:12
  283.3 10.8 %collective-permute-start.22 = (bf16[1,512,256]{1,2,0:T(8,128)(2,1)S(1)}, bf16[1,512,256]{1,2,0:T(8,128)(2,1)S(1)}, u32[]{:S(2)}, u32[]{:S(2)}) collective-permute-start(bf16[1,512,256]{1,2,0:T(8,128)(2,1)S(1)} %broadcast_select_fusion.19), channel_id=1, source_target_pairs={{0,256},{16,272},{32,288},{48,304},{64,320},{80,336},{96,352},{112... | collective-permute-start | bytes 786440 | tf_op jit(solution)/shard_map/ppermute | solution.py:12
  294.1 8.4 %collective-permute-start.23 = (bf16[1,512,256]{1,2,0:T(8,128)(2,1)S(1)}, bf16[1,512,256]{1,2,0:T(8,128)(2,1)S(1)}, u32[]{:S(2)}, u32[]{:S(2)}) collective-permute-start(bf16[1,512,256]{1,2,0:T(8,128)(2,1)S(1)} %broadcast_select_fusion.17), channel_id=1, source_target_pairs={{0,128},{16,144},{32,160},{48,176},{64,192},{80,208},{96,224},{112... | collective-permute-start | bytes 786440 | tf_op jit(solution)/shard_map/ppermute | solution.py:12
  302.6 27.2 %collective-permute-start.24 = (bf16[1,512,256]{1,2,0:T(8,128)(2,1)S(1)}, bf16[1,512,256]{1,2,0:T(8,128)(2,1)S(1)}, u32[]{:S(2)}, u32[]{:S(2)}) collective-permute-start(bf16[1,512,256]{1,2,0:T(8,128)(2,1)S(1)} %broadcast_select_fusion.15), channel_id=1, source_target_pairs={{0,64},{16,80},{32,96},{48,112},{64,0},{80,16},{96,32},{112,48},{1... | collective-permute-start | bytes 786440 | tf_op jit(solution)/shard_map/ppermute | solution.py:12
  329.8 12.6 %collective-permute-start.25 = (bf16[1,512,256]{1,2,0:T(8,128)(2,1)S(1)}, bf16[1,512,256]{1,2,0:T(8,128)(2,1)S(1)}, u32[]{:S(2)}, u32[]{:S(2)}) collective-permute-start(bf16[1,512,256]{1,2,0:T(8,128)(2,1)S(1)} %broadcast_select_fusion.13), channel_id=1, source_target_pairs={{0,32},{16,48},{32,0},{48,16},{64,96},{80,112},{96,64},{112,80},{1... | collective-permute-start | bytes 786440 | tf_op jit(solution)/shard_map/ppermute | solution.py:12
  342.5 11.6 %collective-permute-start.26 = (bf16[1,512,256]{1,2,0:T(8,128)(2,1)S(1)}, bf16[1,512,256]{1,2,0:T(8,128)(2,1)S(1)}, u32[]{:S(2)}, u32[]{:S(2)}) collective-permute-start(bf16[1,512,256]{1,2,0:T(8,128)(2,1)S(1)} %broadcast_select_fusion.11), channel_id=1, source_target_pairs={{0,256},{16,272},{32,288},{48,304},{64,320},{80,336},{96,352},{112... | collective-permute-start | bytes 786440 | tf_op jit(solution)/shard_map/ppermute | solution.py:12
  354.1 9.3 %collective-permute-start.27 = (bf16[1,512,256]{1,2,0:T(8,128)(2,1)S(1)}, bf16[1,512,256]{1,2,0:T(8,128)(2,1)S(1)}, u32[]{:S(2)}, u32[]{:S(2)}) collective-permute-start(bf16[1,512,256]{1,2,0:T(8,128)(2,1)S(1)} %broadcast_select_fusion.9), channel_id=1, source_target_pairs={{0,128},{16,144},{32,160},{48,176},{64,192},{80,208},{96,224},{112... | collective-permute-start | bytes 786440 | tf_op jit(solution)/shard_map/ppermute | solution.py:12
  363.4 25.8 %collective-permute-start.28 = (bf16[1,512,256]{1,2,0:T(8,128)(2,1)S(1)}, bf16[1,512,256]{1,2,0:T(8,128)(2,1)S(1)}, u32[]{:S(2)}, u32[]{:S(2)}) collective-permute-start(bf16[1,512,256]{1,2,0:T(8,128)(2,1)S(1)} %broadcast_select_fusion.7), channel_id=1, source_target_pairs={{0,64},{16,80},{32,96},{48,112},{64,0},{80,16},{96,32},{112,48},{1... | collective-permute-start | bytes 786440 | tf_op jit(solution)/shard_map/ppermute | solution.py:12
  389.3 11.6 %collective-permute-start.29 = (bf16[1,512,256]{1,2,0:T(8,128)(2,1)S(1)}, bf16[1,512,256]{1,2,0:T(8,128)(2,1)S(1)}, u32[]{:S(2)}, u32[]{:S(2)}) collective-permute-start(bf16[1,512,256]{1,2,0:T(8,128)(2,1)S(1)} %broadcast_select_fusion.5), channel_id=1, source_target_pairs={{0,256},{16,272},{32,288},{48,304},{64,320},{80,336},{96,352},{112... | collective-permute-start | bytes 786440 | tf_op jit(solution)/shard_map/ppermute | solution.py:12
  401.0 9.3 %collective-permute-start.30 = (bf16[1,512,256]{1,2,0:T(8,128)(2,1)S(1)}, bf16[1,512,256]{1,2,0:T(8,128)(2,1)S(1)}, u32[]{:S(2)}, u32[]{:S(2)}) collective-permute-start(bf16[1,512,256]{1,2,0:T(8,128)(2,1)S(1)} %broadcast_select_fusion.3), channel_id=1, source_target_pairs={{0,128},{16,144},{32,160},{48,176},{64,192},{80,208},{96,224},{112... | collective-permute-start | bytes 786440 | tf_op jit(solution)/shard_map/ppermute | solution.py:12
  404.9 12.2 %collective-permute-start.16 = (bf16[512,256]{0,1:T(8,128)(2,1)S(1)}, bf16[512,256]{0,1:T(8,128)(2,1)S(1)}, u32[]{:S(2)}, u32[]{:S(2)}) collective-permute-start(bf16[512,256]{0,1:T(8,128)(2,1)S(1)} %get-tuple-element.231), channel_id=1, source_target_pairs={{16,0},{32,16},{48,32},{64,48},{80,64},{96,80},{112,96},{128,112},... | collective-permute-start | bytes 786440 | tf_op jit(solution)/shard_map/ppermute | solution.py:18
  410.3 10.6 %collective-permute-start.31 = (bf16[1,512,256]{1,2,0:T(8,128)(2,1)S(1)}, bf16[1,512,256]{1,2,0:T(8,128)(2,1)S(1)}, u32[]{:S(2)}, u32[]{:S(2)}) collective-permute-start(bf16[1,512,256]{1,2,0:T(8,128)(2,1)S(1)} %broadcast_select_fusion.1), channel_id=1, source_target_pairs={{0,256},{16,272},{32,288},{48,304},{64,320},{80,336},{96,352},{112... | collective-permute-start | bytes 786440 | tf_op jit(solution)/shard_map/ppermute | solution.py:12
where the time goes:
time: 429 us; the launch traced here: 423 us
  waiting for transfers between devices  253 us (59%)
  starting transfers between devices  125 us (29%)
  local copies, waits for them, and re-layouts  24.6 us (6%)
  between operations  10.8 us (3%)
  matrix products  6.08 us (1%)
    ppermute x30, waiting for transfers between devices, from_partner(): return lax.ppermute(value, axis, pairs)  253 us
    ppermute x30, starting transfers between devices, from_partner(): return lax.ppermute(value, axis, pairs)  122 us
    gather x15, local copies, waits for them, and re-layouts, sort_sections(): jnp.take(keys_now, jnp.bitwise_xor(element_ids, 1 << bit_number))  10.5 us
    gather x15, local copies, waits for them, and re-layouts, sort_sections(): section_list.append((bit_number, jnp.take(moved_flags, my_places)))  9.17 us
  transfers between devices with their start and end apart: 32, of which 31 were waited for; matrix products, arithmetic and copies ran while one was open for 6% of the time, Pallas kernels for 0%

commit v1 on v0

v1 whole, which is shorter than its diff:
```python
import jax
import jax.numpy as jnp
from jax import lax
from jax.sharding import PartitionSpec as P

BLK = 512


def passed_along(value, axis, steps):
    count = lax.axis_size(axis)
    first, last = (max(0, -steps), min(count, count - steps))
    return lax.ppermute(value, axis, [(source, source + steps) for source in range(first, last)])


def window_block(query_rows, window, grad_rows, has_prev):
    width = query_rows.shape[1]
    span = query_rows.shape[0]
    scale = width ** (-0.5)
    win_keys = window[:, :width]
    win_values = window[:, width:]
    scores = jnp.dot(query_rows, win_keys.T, preferred_element_type=jnp.float32) * scale
    column = jnp.arange(window.shape[0], dtype=jnp.int32)
    allowed = jnp.logical_or(column >= span, has_prev)
    scores = jnp.where(allowed[None, :], scores, -1e30)
    top = jnp.max(scores, axis=1, keepdims=True)
    expon = jnp.exp(scores - top)
    probs = expon / jnp.sum(expon, axis=1, keepdims=True)
    probs_low = probs.astype(jnp.bfloat16)
    attended = jnp.dot(probs_low, win_values, preferred_element_type=jnp.float32).astype(
        jnp.bfloat16
    )
    grad_probs = jnp.dot(grad_rows, win_values.T, preferred_element_type=jnp.float32)
    delta = jnp.sum(probs * grad_probs, axis=1, keepdims=True)
    grad_scores = (probs * (grad_probs - delta) * scale).astype(jnp.bfloat16)
    grad_query = jnp.dot(grad_scores, win_keys, preferred_element_type=jnp.float32).astype(
        jnp.bfloat16
    )
    grad_key = jnp.dot(grad_scores.T, query_rows, preferred_element_type=jnp.float32)
    grad_value = jnp.dot(probs_low.T, grad_rows, preferred_element_type=jnp.float32)
    window_grads = jnp.concatenate([grad_key, grad_value], axis=1).astype(jnp.bfloat16)
    return (attended, grad_query, window_grads)


def exchange(pieces):
    return lax.all_to_all(pieces, "seq", 0, 0, tiled=True)


def route(blocks, source_of):
    count = source_of.shape[0]
    pieces = blocks.reshape(count, blocks.shape[0] // count, blocks.shape[1])
    held = exchange(pieces)
    return exchange(jnp.take(held, source_of, axis=0)).reshape(blocks.shape)


def body(queries, keys, values, grad_out, block_perm):
    width = queries.shape[1]
    seq_index = lax.axis_index("seq")
    pair = jnp.concatenate([keys, values], axis=1)
    perm_row = block_perm[0]
    ids = jnp.arange(perm_row.shape[0], dtype=jnp.int32)
    inverse = jnp.sum(jnp.where(perm_row[None, :] == ids[:, None], ids[None, :], 0), axis=1)
    far_pair = route(pair, perm_row)
    prev_pair = passed_along(pair, "seq", 1)
    window = jnp.concatenate([prev_pair, pair, far_pair], axis=0)
    attended, grad_query, window_grads = window_block(queries, window, grad_out, seq_index > 0)
    far_back = route(window_grads[2 * BLK :], inverse)
    prev_back = passed_along(window_grads[:BLK], "seq", -1)
    total = (
        window_grads[BLK : 2 * BLK].astype(jnp.float32)
        + prev_back.astype(jnp.float32)
        + far_back.astype(jnp.float32)
    ).astype(jnp.bfloat16)
    return attended, grad_query, total[:, :width], total[:, width:]


def solution(mesh):
    placed = (
        P("seq", "head"),
        P("seq", "head"),
        P("seq", "head"),
        P("seq", "head"),
        P("head", None),
    )
    return jax.shard_map(
        body,
        mesh=mesh,
        in_specs=placed,
        out_specs=(P("seq", "head"), P("seq", "head"), P("seq", "head"), P("seq", "head")),
        check_vma=False,
    )
```

time: 429 us -> 132 us (0.31); the launches traced: 423 us -> 132 us
  waiting for transfers between devices: 253 us -> 70.9 us
  starting transfers between devices: 125 us -> 35.6 us
  local copies, waits for them, and re-layouts: 24.6 us -> 9.83 us
  between operations: 10.8 us -> 0.91 us
    ppermute x30 -> x0, waiting for transfers between devices: 253 us -> none  [from_partner(): return lax.ppermute(value, axis, pairs)]
    ppermute x30 -> x0, starting transfers between devices: 122 us -> none  [from_partner(): return lax.ppermute(value, axis, pairs)]
    all_to_all x0 -> x4, waiting for transfers between devices: none -> 64.7 us  [exchange(): return lax.all_to_all(pieces, 'seq', 0, 0, tiled=True)]
    all_to_all x0 -> x4, starting transfers between devices: none -> 30.5 us  [exchange(): return lax.all_to_all(pieces, 'seq', 0, 0, tiled=True)]
    gather x30 -> x2, local copies, waits for them, and re-layouts: 19.6 us -> 2.08 us  [route(): return exchange(jnp.take(held, source_of, axis=0)).reshape(blocks.shape)]
    ppermute x2, waiting for transfers between devices: 0.5 us -> 6.23 us  [passed_along(): lax.ppermute(value, axis, [(source, source + steps) for source in range(f...]
  transfers between devices with their start and end apart: 32 -> 6, of which waited for: 31 -> 5; matrix products, arithmetic and copies ran while one was open for 6% -> 4% of each run, Pallas kernels for 0% -> 0%
where the time goes in v1:
time: 132 us
  waiting for transfers between devices  70.9 us (54%)
  starting transfers between devices  35.6 us (27%)
  local copies, waits for them, and re-layouts  9.83 us (7%)
  other arithmetic  7.3 us (6%)
  matrix products  6.92 us (5%)
    all_to_all x4, waiting for transfers between devices, exchange(): return lax.all_to_all(pieces, 'seq', 0, 0, tiled=True)  64.7 us
    all_to_all x4, starting transfers between devices, exchange(): return lax.all_to_all(pieces, 'seq', 0, 0, tiled=True)  30.5 us
    ppermute x2, waiting for transfers between devices, passed_along(): lax.ppermute(value, axis, [(source, source + steps) for source in range(f...  6.23 us
    ppermute x2, starting transfers between devices, passed_along(): lax.ppermute(value, axis, [(source, source + steps) for source in range(f...  5.13 us
    unnamed x25, local copies, waits for them, and re-layouts  5.11 us
  transfers between devices with their start and end apart: 6, of which 5 were waited for; matrix products, arithmetic and copies ran while one was open for 4% of the time, Pallas kernels for 0%

profile of v1, /device:TPU:6, one launch (start us, length us, event | category | flops | bytes accessed | tf_op | source)
XLA Modules:
  0.0 131.5 jit_solution(4233284851448310550)
XLA Ops:
  0.6 0.0 copy-start
  0.6 0.0 copy-start.9
  0.7 1.6 %constant_dynamic-update-slice_fusion.1 = bf16[512,256]{1,0:T(8,128)(2,1)} fusion(bf16[512,128]{1,0:T(8,128)(2,1)} %param.8), kind=kLoop, calls=%fused_computation.41 | loop fusion | bytes 262144
  2.3 1.6 %constant_dynamic-update-slice_fusion = bf16[512,256]{1,0:T(8,128)(2,1)} fusion(bf16[512,256]{1,0:T(8,128)(2,1)} %constant_dynamic-update-slice_fusion.1, bf16[512,128]{1,0:T(8,128)(2,1)} %param.9), kind=kLoop, calls=%fused_computation.40 | loop fusion | bytes 262144 | tf_op jit(solution)/shard_map/concatenate | solution.py:58
  3.9 15.5 %all-to-all-start = ((bf16[32,16,256]{2,1,0:T(8,128)(2,1)}), bf16[32,16,256]{2,1,0:T(8,128)(2,1)S(1)}, u32[]{:S(2)}, u32[]{:S(2)}) async-start(bf16[32,16,256]{2,1,0:T(8,128)(2,1)} %bitcast.1), calls=%async_computation | async-start | bytes 524288 | tf_op jit(solution)/shard_map/all_to_all | solution.py:45
  19.4 0.7 compare_select_fusion.1
  20.1 0.7 compare_and_fusion.1
  20.7 18.2 %all-to-all-done = bf16[32,16,256]{2,1,0:T(8,128)(2,1)S(1)} async-done(((bf16[32,16,256]{2,1,0:T(8,128)(2,1)}), bf16[32,16,256]{2,1,0:T(8,128)(2,1)S(1)}, u32[]{:S(2)}, u32[]{:S(2)}) %all-to-all-start) | async-done | bytes 262176 | tf_op jit(solution)/shard_map/all_to_all | solution.py:45
  38.9 0.6 gather_fusion
  39.5 0.8 broadcast_select_fusion.1
  40.3 5.1 %all-to-all-start.1 = ((bf16[32,16,256]{2,1,0:T(8,128)(2,1)}), bf16[32,16,256]{2,1,0:T(8,128)(2,1)S(1)}, u32[]{:S(2)}, u32[]{:S(2)}) async-start(bf16[32,16,256]{2,1,0:T(8,128)(2,1)} %broadcast_select_fusion.1), calls=%async_computation.1 | async-start | bytes 524288 | tf_op jit(solution)/shard_map/all_to_all | solution.py:45
  45.5 3.7 %collective-permute-start = (bf16[512,256]{1,0:T(8,128)(2,1)}, bf16[512,256]{1,0:T(8,128)(2,1)S(1)}, u32[]{:S(2)}, u32[]{:S(2)}) collective-permute-start(bf16[512,256]{1,0:T(8,128)(2,1)} %constant_dynamic-update-slice_fusion), channel_id=1, source_target_pairs={{0,16},{16,32},{32,48},{48,64},{64,80},{80,96},{96,112},{112,128},... | collective-permute-start | bytes 786440 | tf_op jit(solution)/shard_map/ppermute | solution.py:12
  49.2 6.2 %collective-permute-done = bf16[512,256]{1,0:T(8,128)(2,1)S(1)} collective-permute-done((bf16[512,256]{1,0:T(8,128)(2,1)}, bf16[512,256]{1,0:T(8,128)(2,1)S(1)}, u32[]{:S(2)}, u32[]{:S(2)}) %collective-permute-start) | collective-permute-done | bytes 262176 | tf_op jit(solution)/shard_map/ppermute | solution.py:12
  55.4 12.9 %all-to-all-done.1 = bf16[32,16,256]{2,1,0:T(8,128)(2,1)S(1)} async-done(((bf16[32,16,256]{2,1,0:T(8,128)(2,1)}), bf16[32,16,256]{2,1,0:T(8,128)(2,1)S(1)}, u32[]{:S(2)}, u32[]{:S(2)}) %all-to-all-start.1) | async-done | bytes 262176 | tf_op jit(solution)/shard_map/all_to_all | solution.py:45
  68.4 1.0 pad_maximum_fusion
  69.4 0.0 copy-done.9
  69.4 0.0 copy-start.5
  69.4 1.2 fusion.16
  70.6 0.5 fusion.4
  71.1 0.0 copy-done.5
  71.1 0.0 copy-done
  71.1 0.7 fusion.1
  71.9 0.7 convolution_convert_fusion
  72.6 0.0 copy-start.7
  72.6 0.9 fusion.3
  73.5 0.0 copy-start.1
  73.5 1.2 copy-done.1
  74.7 0.0 copy-start.10
  74.7 0.6 convolution_convert_fusion.1
  75.3 0.0 copy-done.7
  75.3 0.0 copy-start.3
  75.3 0.8 copy-done.3
  76.1 0.7 fusion.10
  76.8 0.9 copy.15
  77.7 4.7 %all-to-all-start.2 = ((bf16[32,16,256]{2,1,0:T(8,128)(2,1)}), bf16[32,16,256]{2,1,0:T(8,128)(2,1)}, u32[]{:S(2)}, u32[]{:S(2)}) async-start(bf16[32,16,256]{2,1,0:T(8,128)(2,1)} %bitcast.30), calls=%async_computation.2 | async-start | bytes 524288 | tf_op jit(solution)/shard_map/all_to_all | solution.py:45
  82.4 0.0 copy-done.10
  82.4 0.1 select_reduce_fusion
  82.5 18.8 %all-to-all-done.2 = bf16[32,16,256]{2,1,0:T(8,128)(2,1)} async-done(((bf16[32,16,256]{2,1,0:T(8,128)(2,1)}), bf16[32,16,256]{2,1,0:T(8,128)(2,1)}, u32[]{:S(2)}, u32[]{:S(2)}) %all-to-all-start.2) | async-done | bytes 262176 | tf_op jit(solution)/shard_map/all_to_all | solution.py:45
  101.3 1.5 %gather_fusion.1 = bf16[32,16,256]{2,1,0:T(8,128)(2,1)S(1)} fusion(bf16[32,16,256]{2,1,0:T(8,128)(2,1)} %all-to-all-done.2, s32[1024]{0:T(1024)S(1)} %pad_clamp_fusion), kind=kCustom, calls=%fused_computation.1.clone | custom fusion | bytes 524416 | tf_op jit(solution)/shard_map/jit(_take)/gather | solution.py:52
  102.8 0.8 broadcast_select_fusion
  103.6 5.1 %all-to-all-start.3 = ((bf16[32,16,256]{2,1,0:T(8,128)(2,1)}), bf16[32,16,256]{2,1,0:T(8,128)(2,1)S(1)}, u32[]{:S(2)}, u32[]{:S(2)}) async-start(bf16[32,16,256]{2,1,0:T(8,128)(2,1)} %broadcast_select_fusion), calls=%async_computation.3 | async-start | bytes 524288 | tf_op jit(solution)/shard_map/all_to_all | solution.py:45
  108.8 0.0 copy-start.2
  108.8 0.0 copy-start.6
  108.8 1.4 %collective-permute-start.1 = (bf16[512,256]{0,1:T(8,128)(2,1)}, bf16[512,256]{0,1:T(8,128)(2,1)}, u32[]{:S(2)}, u32[]{:S(2)}) collective-permute-start(bf16[512,256]{0,1:T(8,128)(2,1)} %get-tuple-element.17), channel_id=1, source_target_pairs={{16,0},{32,16},{48,32},{64,48},{80,64},{96,80},{112,96},{128,112},... | collective-permute-start | bytes 786440 | tf_op jit(solution)/shard_map/ppermute | solution.py:12
  110.2 2.3 %convolution_convert_fusion.3 = bf16[512,128]{1,0:T(8,128)(2,1)} fusion(bf16[1536,256]{1,0:T(8,128)(2,1)} %copy-done.5, f32[1536,512]{1,0:T(8,128)S(1)} %get-tuple-element.22, f32[512]{0:T(512)S(1)} %fusion.4, f32[512]{0:T(512)S(1)} %get-tuple-element.21), kind=kOutput, calls=%fused_computation.17 | convolution fusion | flops 203751424 | bytes 3674112 | tf_op jit(solution)/shard_map/dot_general | solution.py:29
  112.6 0.0 copy-done.2
  112.6 0.0 copy-done.6
  112.6 0.0 copy-start.4
  112.6 0.0 copy-start.8
  112.6 1.3 convolution_convert_fusion.2
  113.8 14.8 %all-to-all-done.3 = bf16[32,16,256]{2,1,0:T(8,128)(2,1)S(1)} async-done(((bf16[32,16,256]{2,1,0:T(8,128)(2,1)}), bf16[32,16,256]{2,1,0:T(8,128)(2,1)S(1)}, u32[]{:S(2)}, u32[]{:S(2)}) %all-to-all-start.3) | async-done | bytes 262176 | tf_op jit(solution)/shard_map/all_to_all | solution.py:45
  128.6 0.1 bitcast_convert_fusion.3
  128.7 0.2 copy.16
  128.9 0.0 collective-permute-done.1
  128.9 0.0 copy-done.4
  128.9 0.0 copy-done.8
  128.9 1.1 add_convert_fusion
  130.0 0.8 copy.17
  130.8 0.8 copy.18
  (6 shorter events, 0.1 us)
Async XLA Ops:
  0.6 70.5 %copy-start = (bf16[512,128]{1,0:T(8,128)(2,1)S(1)}, bf16[512,128]{1,0:T(8,128)(2,1)}, u32[]{:S(2)}) copy-start(bf16[512,128]{1,0:T(8,128)(2,1)} %param.10) | copy-start | bytes 393220
  0.6 68.8 %copy-start.9 = (bf16[512,128]{1,0:T(8,128)(2,1)S(1)}, bf16[512,128]{1,0:T(8,128)(2,1)}, u32[]{:S(2)}) copy-start(bf16[512,128]{1,0:T(8,128)(2,1)} %param.7) | copy-start | bytes 393220
  3.9 35.1 %all-to-all-start = ((bf16[32,16,256]{2,1,0:T(8,128)(2,1)}), bf16[32,16,256]{2,1,0:T(8,128)(2,1)S(1)}, u32[]{:S(2)}, u32[]{:S(2)}) async-start(bf16[32,16,256]{2,1,0:T(8,128)(2,1)} %bitcast.1), calls=%async_computation | async-start | bytes 524288 | tf_op jit(solution)/shard_map/all_to_all | solution.py:45
  40.3 28.1 %all-to-all-start.1 = ((bf16[32,16,256]{2,1,0:T(8,128)(2,1)}), bf16[32,16,256]{2,1,0:T(8,128)(2,1)S(1)}, u32[]{:S(2)}, u32[]{:S(2)}) async-start(bf16[32,16,256]{2,1,0:T(8,128)(2,1)} %broadcast_select_fusion.1), calls=%async_computation.1 | async-start | bytes 524288 | tf_op jit(solution)/shard_map/all_to_all | solution.py:45
  45.5 10.0 %collective-permute-start = (bf16[512,256]{1,0:T(8,128)(2,1)}, bf16[512,256]{1,0:T(8,128)(2,1)S(1)}, u32[]{:S(2)}, u32[]{:S(2)}) collective-permute-start(bf16[512,256]{1,0:T(8,128)(2,1)} %constant_dynamic-update-slice_fusion), channel_id=1, source_target_pairs={{0,16},{16,32},{32,48},{48,64},{64,80},{80,96},{96,112},{112,128},... | collective-permute-start | bytes 786440 | tf_op jit(solution)/shard_map/ppermute | solution.py:12
  69.4 1.7 %copy-start.5 = (bf16[1536,256]{1,0:T(8,128)(2,1)}, bf16[1536,256]{1,0:T(8,128)(2,1)S(1)}, u32[]{:S(2)}) copy-start(bf16[1536,256]{1,0:T(8,128)(2,1)S(1)} %pad_maximum_fusion) | copy-start | bytes 2359300
  72.6 2.7 %copy-start.7 = (bf16[1536,128]{0,1:T(8,128)(2,1)}, bf16[1536,128]{0,1:T(8,128)(2,1)S(1)}, u32[]{:S(2)}) copy-start(bf16[1536,128]{0,1:T(8,128)(2,1)S(1)} %convolution_convert_fusion) | copy-start | bytes 1179652
  73.5 1.2 copy-start.1
  74.7 7.7 %copy-start.10 = (s32[1,32]{1,0:T(1,128)S(1)}, s32[1,32]{1,0:T(1,128)}, u32[]{:S(2)}) copy-start(s32[1,32]{1,0:T(1,128)} %param.11) | copy-start | bytes 388
  75.3 0.8 copy-start.3
  77.7 23.6 %all-to-all-start.2 = ((bf16[32,16,256]{2,1,0:T(8,128)(2,1)}), bf16[32,16,256]{2,1,0:T(8,128)(2,1)}, u32[]{:S(2)}, u32[]{:S(2)}) async-start(bf16[32,16,256]{2,1,0:T(8,128)(2,1)} %bitcast.30), calls=%async_computation.2 | async-start | bytes 524288 | tf_op jit(solution)/shard_map/all_to_all | solution.py:45
  103.6 25.0 %all-to-all-start.3 = ((bf16[32,16,256]{2,1,0:T(8,128)(2,1)}), bf16[32,16,256]{2,1,0:T(8,128)(2,1)S(1)}, u32[]{:S(2)}, u32[]{:S(2)}) async-start(bf16[32,16,256]{2,1,0:T(8,128)(2,1)} %broadcast_select_fusion), calls=%async_computation.3 | async-start | bytes 524288 | tf_op jit(solution)/shard_map/all_to_all | solution.py:45
  108.8 3.8 %copy-start.2 = (bf16[512,1536]{0,1:T(8,128)(2,1)S(1)}, bf16[512,1536]{0,1:T(8,128)(2,1)}, u32[]{:S(2)}) copy-start(bf16[512,1536]{0,1:T(8,128)(2,1)} %copy-done.1) | copy-start | bytes 4718596
  108.8 3.8 %copy-start.6 = (bf16[1536,256]{1,0:T(8,128)(2,1)S(1)}, bf16[1536,256]{1,0:T(8,128)(2,1)}, u32[]{:S(2)}) copy-start(bf16[1536,256]{1,0:T(8,128)(2,1)} %copy-done.5) | copy-start | bytes 2359300
  108.8 20.1 %collective-permute-start.1 = (bf16[512,256]{0,1:T(8,128)(2,1)}, bf16[512,256]{0,1:T(8,128)(2,1)}, u32[]{:S(2)}, u32[]{:S(2)}) collective-permute-start(bf16[512,256]{0,1:T(8,128)(2,1)} %get-tuple-element.17), channel_id=1, source_target_pairs={{16,0},{32,16},{48,32},{64,48},{80,64},{96,80},{112,96},{128,112},... | collective-permute-start | bytes 786440 | tf_op jit(solution)/shard_map/ppermute | solution.py:12
  112.6 16.3 %copy-start.4 = (bf16[1536,128]{0,1:T(8,128)(2,1)S(1)}, bf16[1536,128]{0,1:T(8,128)(2,1)}, u32[]{:S(2)}) copy-start(bf16[1536,128]{0,1:T(8,128)(2,1)} %copy-done.3) | copy-start | bytes 1179652
  112.6 16.3 %copy-start.8 = (bf16[1536,128]{0,1:T(8,128)(2,1)S(1)}, bf16[1536,128]{0,1:T(8,128)(2,1)}, u32[]{:S(2)}) copy-start(bf16[1536,128]{0,1:T(8,128)(2,1)} %copy-done.7) | copy-start | bytes 1179652

commit v2 on v1

v2 whole, which is shorter than its diff:
```python
import jax
import jax.numpy as jnp
from jax import lax
from jax.experimental import pallas as pl
from jax.experimental.pallas import tpu as pltpu
from jax.sharding import PartitionSpec as P

MESH = pl.DeviceIdType.MESH
AXIS = "seq"
ALONG_Z = 8


def dot_nt(left, right):
    return lax.dot_general(left, right, (((1,), (1,)), ((), ())), preferred_element_type=jnp.float32)


def dot_tn(left, right):
    return lax.dot_general(left, right, (((0,), (0,)), ((), ())), preferred_element_type=jnp.float32)


def dot_nn(left, right):
    return jnp.dot(left, right, preferred_element_type=jnp.float32)


def target(step, me, count):
    ring = step // (count // ALONG_Z)
    turn = (step + 1) % (count // ALONG_Z)
    along = (ALONG_Z // 2 + (1 - 2 * (ring % 2)) * ((ring + 1) // 2)) % ALONG_Z
    place = (me % ALONG_Z + along) % ALONG_Z
    row = (me // ALONG_Z + turn) % (count // ALONG_Z)
    return row * ALONG_Z + place


def rows_of(index, size):
    return pl.ds(pl.multiple_of(index * size, size), size)


def await_bytes(ref, sem):
    pltpu.make_async_copy(ref, ref, sem).wait()


def kernel(
    count, perm_ref, q_hbm, k_hbm, v_hbm, g_hbm, o_ref, dq_ref, dk_ref, dv_ref,
    inv, kv, qd, held_kv, held_qd, sorted_kv, sorted_qd, far_kv, far_qd, prev_kv, next_qd,
    stats, in_sem, send_sem, recv_sem,
):
    me = lax.axis_index(AXIS)
    span, width = q_hbm.shape
    piece = span // count
    scale = width ** (-0.5)
    others = count - 1

    loads = [
        pltpu.make_async_copy(k_hbm, kv.at[0], in_sem.at[0]),
        pltpu.make_async_copy(v_hbm, kv.at[1], in_sem.at[1]),
        pltpu.make_async_copy(q_hbm, qd.at[0], in_sem.at[2]),
        pltpu.make_async_copy(g_hbm, qd.at[1], in_sem.at[3]),
    ]
    for load in loads:
        load.start()

    barrier = pltpu.get_barrier_semaphore()

    def greet(step, carry):
        pl.semaphore_signal(
            barrier, inc=1, device_id={AXIS: target(step, me, count)}, device_id_type=MESH
        )
        return carry

    lax.fori_loop(0, others, greet, 0)

    def invert(block, carry):
        found = jnp.int32(0)
        for query in range(count):
            found = jnp.where(perm_ref[0, query] == block, query, found)
        inv[block] = found
        return carry

    lax.fori_loop(0, count, invert, 0)

    for load in loads:
        load.wait()
    pl.semaphore_wait(barrier, others)

    def spread(source, held, stream):
        def issue(step, carry):
            to = target(step, me, count)
            pltpu.make_async_remote_copy(
                src_ref=source.at[:, rows_of(to, piece), :],
                dst_ref=held.at[me],
                send_sem=send_sem.at[stream],
                recv_sem=recv_sem.at[stream],
                device_id={AXIS: to},
                device_id_type=MESH,
            ).start()
            return carry

        lax.fori_loop(0, others, issue, 0)

    def shift(source, landing, to, stream):
        return pltpu.make_async_remote_copy(
            src_ref=source,
            dst_ref=landing,
            send_sem=send_sem.at[stream],
            recv_sem=recv_sem.at[stream],
            device_id={AXIS: to},
            device_id_type=MESH,
        )

    def deliver(held, arranged, landing, index_of, stream_in, stream_out):
        held[me] = held_own[stream_in]
        await_bytes(held.at[pl.ds(0, others)], recv_sem.at[stream_in])

        def reorder(block, carry):
            arranged[block] = held[index_of(block)]
            return carry

        lax.fori_loop(0, count, reorder, 0)

        def issue(step, carry):
            to = target(step, me, count)
            pltpu.make_async_remote_copy(
                src_ref=arranged.at[to],
                dst_ref=landing.at[:, rows_of(me, piece), :],
                send_sem=send_sem.at[stream_out],
                recv_sem=recv_sem.at[stream_out],
                device_id={AXIS: to},
                device_id_type=MESH,
            ).start()
            return carry

        lax.fori_loop(0, others, issue, 0)
        landing[:, rows_of(me, piece), :] = arranged[me]

    shift_kv = shift(kv, prev_kv, (me + 1) % count, 2)
    shift_qd = shift(qd, next_qd, (me + count - 1) % count, 3)
    held_own = {0: kv[:, rows_of(me, piece), :], 1: qd[:, rows_of(me, piece), :]}

    spread(kv, held_kv, 0)

    @pl.when(me < others)
    def _():
        shift_kv.start()

    spread(qd, held_qd, 1)

    @pl.when(me > 0)
    def _():
        shift_qd.start()

    @pl.when(me == 0)
    def _():
        prev_kv[...] = jnp.zeros_like(prev_kv)

    @pl.when(me == others)
    def _():
        next_qd[...] = jnp.zeros_like(next_qd)

    deliver(held_kv, sorted_kv, far_kv, lambda block: perm_ref[0, block], 0, 4)
    deliver(held_qd, sorted_qd, far_qd, lambda block: inv[block], 1, 5)

    @pl.when(me > 0)
    def _():
        shift_kv.wait_recv()

    await_bytes(held_kv.at[pl.ds(0, others)], recv_sem.at[4])

    query_rows = qd[0]
    grad_rows = qd[1]
    key_sets = [prev_kv[0], kv[0], far_kv[0]]
    value_sets = [prev_kv[1], kv[1], far_kv[1]]
    scores = [dot_nt(keys, query_rows) * scale for keys in key_sets]
    scores[0] = jnp.where(me > 0, scores[0], -1e30)
    top = jnp.max(jnp.maximum(jnp.maximum(scores[0], scores[1]), scores[2]), axis=0, keepdims=True)
    expons = [jnp.exp(part - top) for part in scores]
    total = sum(jnp.sum(part, axis=0, keepdims=True) for part in expons)
    inverse_total = 1.0 / total
    probs = [part * inverse_total for part in expons]
    grad_probs = [dot_nt(values, grad_rows) for values in value_sets]
    delta = sum(
        jnp.sum(part * grads, axis=0, keepdims=True) for part, grads in zip(probs, grad_probs)
    )
    stats[me] = jnp.concatenate([top + jnp.log(total), delta], axis=0)
    attended = jnp.zeros((span, width), jnp.float32)
    grad_query = jnp.zeros((span, width), jnp.float32)
    for index in range(3):
        low = probs[index].astype(jnp.bfloat16)
        grad_scores = (probs[index] * (grad_probs[index] - delta) * scale).astype(jnp.bfloat16)
        attended += dot_tn(low, value_sets[index])
        grad_query += dot_tn(grad_scores, key_sets[index])
        if index == 1:
            grad_key = dot_nn(grad_scores, query_rows)
            grad_value = dot_nn(low, grad_rows)
    o_ref[...] = attended.astype(jnp.bfloat16)
    dq_ref[...] = grad_query.astype(jnp.bfloat16)

    def tell(step, carry):
        pltpu.make_async_remote_copy(
            src_ref=stats.at[me],
            dst_ref=stats.at[me],
            send_sem=send_sem.at[6],
            recv_sem=recv_sem.at[6],
            device_id={AXIS: target(step, me, count)},
            device_id_type=MESH,
        ).start()
        return carry

    lax.fori_loop(0, others, tell, 0)

    @pl.when(me < others)
    def _():
        shift_qd.wait_recv()

    await_bytes(held_qd.at[pl.ds(0, others)], recv_sem.at[5])
    await_bytes(stats.at[pl.ds(0, others)], recv_sem.at[6])

    known = {
        0: jnp.where(me < others, stats[(me + 1) % count], 0.0),
        1: stats[inv[me]],
    }
    for index, arrived in ((0, next_qd), (1, far_qd)):
        part_q = arrived[0]
        part_g = arrived[1]
        part = jnp.exp(dot_nt(kv[0], part_q) * scale - known[index][0:1])
        part_probs = dot_nt(kv[1], part_g)
        low = part.astype(jnp.bfloat16)
        grad_scores = (part * (part_probs - known[index][1:2]) * scale).astype(jnp.bfloat16)
        grad_key += dot_nn(grad_scores, part_q)
        grad_value += dot_nn(low, part_g)
    dk_ref[...] = grad_key.astype(jnp.bfloat16)
    dv_ref[...] = grad_value.astype(jnp.bfloat16)

    for stream, held in ((0, held_kv), (1, held_qd), (4, held_kv), (5, held_qd), (6, stats)):
        await_bytes(held.at[pl.ds(0, others)], send_sem.at[stream])

    @pl.when(me < others)
    def _():
        shift_kv.wait_send()

    @pl.when(me > 0)
    def _():
        shift_qd.wait_send()


def body(queries, keys, values, grad_out, block_perm):
    span, width = queries.shape
    count = lax.axis_size(AXIS)
    piece = span // count
    pair = pltpu.VMEM((2, span, width), jnp.bfloat16)
    pieces = pltpu.VMEM((count, 2, piece, width), jnp.bfloat16)
    in_place = pl.BlockSpec(memory_space=pl.ANY)
    in_vmem = pl.BlockSpec(memory_space=pltpu.VMEM)

    def run(*refs):
        kernel(count, *refs)

    return pl.pallas_call(
        run,
        out_shape=(jax.ShapeDtypeStruct((span, width), jnp.bfloat16),) * 4,
        in_specs=[pl.BlockSpec(memory_space=pltpu.SMEM), in_place, in_place, in_place, in_place],
        out_specs=(in_vmem,) * 4,
        scratch_shapes=[
            pltpu.SMEM((count,), jnp.int32),
            pair, pair, pieces, pieces, pieces, pieces, pair, pair, pair, pair,
            pltpu.VMEM((count, 2, span), jnp.float32),
            pltpu.SemaphoreType.DMA((4,)),
            pltpu.SemaphoreType.DMA((7,)),
            pltpu.SemaphoreType.DMA((7,)),
        ],
        compiler_params=pltpu.CompilerParams(
            collective_id=0, has_side_effects=True, vmem_limit_bytes=60 << 20
        ),
    )(block_perm, queries, keys, values, grad_out)


def solution(mesh):
    placed = (
        P("seq", "head"),
        P("seq", "head"),
        P("seq", "head"),
        P("seq", "head"),
        P("head", None),
    )
    return jax.shard_map(
        body,
        mesh=mesh,
        in_specs=placed,
        out_specs=(P("seq", "head"), P("seq", "head"), P("seq", "head"), P("seq", "head")),
        check_vma=False,
    )
```

time: 132 us -> 87.3 us (0.66)
  Pallas kernels: 0 us -> 82.3 us
  waiting for transfers between devices: 70.9 us -> 0 us
  starting transfers between devices: 35.6 us -> 0 us
  other arithmetic: 7.3 us -> 0 us
  matrix products: 6.92 us -> 0 us
  local copies, waits for them, and re-layouts: 9.83 us -> 4.16 us
    pallas_call x0 -> x1, Pallas kernels: none -> 82.3 us  [body(): pl.pallas_call(run, out_shape=(jax.ShapeDtypeStruct((span, width), jnp.bf...]
    all_to_all x4 -> x0, waiting for transfers between devices: 64.7 us -> none  [exchange(): return lax.all_to_all(pieces, 'seq', 0, 0, tiled=True)]
    all_to_all x4 -> x0, starting transfers between devices: 30.5 us -> none  [exchange(): return lax.all_to_all(pieces, 'seq', 0, 0, tiled=True)]
    dot_general x6 -> x0, matrix products: 6.92 us -> none  [the longest x1 2.34 us: window_block(): jnp.dot(probs_low, win_values, preferred_element_type=jnp.float32)]
    ppermute x2 -> x0, waiting for transfers between devices: 6.23 us -> none  [passed_along(): lax.ppermute(value, axis, [(source, source + steps) for source in range(f...]
    ppermute x2 -> x0, starting transfers between devices: 5.13 us -> none  [passed_along(): lax.ppermute(value, axis, [(source, source + steps) for source in range(f...]
    select_n x4 -> x0, other arithmetic: 2.3 us -> none  [route(): return exchange(jnp.take(held, source_of, axis=0)).reshape(blocks.shape)]
    gather x2 -> x0, local copies, waits for them, and re-layouts: 2.08 us -> none  [route(): return exchange(jnp.take(held, source_of, axis=0)).reshape(blocks.shape)]
  transfers between devices with their start and end apart: 6 -> 0, of which waited for: 5 -> 0; matrix products, arithmetic and copies ran while one was open for 4% -> 0% of each run, Pallas kernels for 0% -> 0%
where the time goes in v2:
time: 87.3 us; the launch traced here: 87.1 us
  Pallas kernels  82.3 us (94%)
  local copies, waits for them, and re-layouts  4.16 us (5%)
    pallas_call x1, Pallas kernels, body(): pl.pallas_call(run, out_shape=(jax.ShapeDtypeStruct((span, width), jnp.bf...  82.3 us
    unnamed x10, local copies, waits for them, and re-layouts  4.16 us

profile of v2, /device:TPU:6, one launch (start us, length us, event | category | flops | bytes accessed | tf_op | source)
XLA Modules:
  0.0 87.1 jit_solution(16620562969083190990)
XLA Ops:
  0.6 82.3 %shard_map.84 = (bf16[512,128]{1,0:T(8,128)(2,1)}, bf16[512,128]{1,0:T(8,128)(2,1)}, bf16[512,128]{1,0:T(8,128)(2,1)}, bf16[512,128]{1,0:T(8,128)(2,1)}) custom-call(s32[1,32]{1,0:T(1,128)} %refs_0_.1, bf16[512,128]{1,0:T(8,128)(2,1)} %refs_1_.1, bf16[512,128]{1,0:T(8,128)(2,1)} %refs_2_.1, bf16[512,128]{1,0:T(8,128)(2,1)} %refs_3_.1, bf16[512,128]{1,0:T(8,128)(2,1)} %refs_4_.1), custom_call_target="tpu_custom_call" | custom-call | tf_op jit(solution)/shard_map/pallas_call | solution.py:257
  83.0 0.0 copy-start.2
  83.0 1.6 %copy.13 = bf16[512,128]{1,0:T(8,128)(2,1)} copy(bf16[512,128]{1,0:T(8,128)(2,1)} %get-tuple-element.8) | data formatting | bytes 262144
  84.6 0.0 copy-done.2
  84.6 0.0 copy-start.1
  84.6 0.7 copy.14
  85.2 0.3 copy-done.1
  85.5 0.0 copy-start
  85.5 0.7 copy.15
  86.2 0.3 copy-done
  86.5 0.7 copy.16
Async XLA Ops:
  83.0 1.6 %copy-start.2 = (bf16[512,128]{1,0:T(8,128)(2,1)S(1)}, bf16[512,128]{1,0:T(8,128)(2,1)}, u32[]{:S(2)}) copy-start(bf16[512,128]{1,0:T(8,128)(2,1)} %get-tuple-element.9) | copy-start | bytes 393220
  84.6 1.0 %copy-start.1 = (bf16[512,128]{1,0:T(8,128)(2,1)S(1)}, bf16[512,128]{1,0:T(8,128)(2,1)}, u32[]{:S(2)}) copy-start(bf16[512,128]{1,0:T(8,128)(2,1)} %get-tuple-element.10) | copy-start | bytes 393220
  85.5 1.0 %copy-start = (bf16[512,128]{1,0:T(8,128)(2,1)S(1)}, bf16[512,128]{1,0:T(8,128)(2,1)}, u32[]{:S(2)}) copy-start(bf16[512,128]{1,0:T(8,128)(2,1)} %get-tuple-element.11) | copy-start | bytes 393220

commit v3 on v2

v3 whole, which is shorter than its diff:
```python
import jax
import jax.numpy as jnp
from jax import lax
from jax.experimental import pallas as pl
from jax.experimental.pallas import tpu as pltpu
from jax.sharding import PartitionSpec as P

MESH = pl.DeviceIdType.MESH
AXIS = "seq"
ALONG_Z = 8


def dot_nt(left, right):
    return lax.dot_general(left, right, (((1,), (1,)), ((), ())), preferred_element_type=jnp.float32)


def dot_tn(left, right):
    return lax.dot_general(left, right, (((0,), (0,)), ((), ())), preferred_element_type=jnp.float32)


def dot_nn(left, right):
    return jnp.dot(left, right, preferred_element_type=jnp.float32)


def target(step, me, count):
    ring = step // (count // ALONG_Z)
    turn = (step + 1) % (count // ALONG_Z)
    along = (ALONG_Z // 2 + (1 - 2 * (ring % 2)) * ((ring + 1) // 2)) % ALONG_Z
    place = (me % ALONG_Z + along) % ALONG_Z
    row = (me // ALONG_Z + turn) % (count // ALONG_Z)
    return row * ALONG_Z + place


def rows_of(index, size):
    return pl.ds(pl.multiple_of(index * size, size), size)


def await_bytes(ref, sem):
    pltpu.make_async_copy(ref, ref, sem).wait()


def kernel(
    count, perm_hbm, q_hbm, k_hbm, v_hbm, g_hbm, o_ref, dq_ref, dk_ref, dv_ref,
    perm_ref, inv, kv, qd, held_kv, held_qd, sorted_kv, sorted_qd, far_kv, far_qd, prev_kv, next_qd,
    full_stats, next_stats, part_stats, held_stats, sorted_stats, far_stats,
    in_sem, send_sem, recv_sem, up_sem, down_sem,
):
    me = lax.axis_index(AXIS)
    span, width = q_hbm.shape
    piece = span // count
    scale = width ** (-0.5)
    others = count - 1
    rows = count // ALONG_Z
    place = me % ALONG_Z
    row = me // ALONG_Z
    last = ALONG_Z - 1
    lanes = 128
    stat_rows = 2 * span // lanes
    stride = count // stat_rows

    def signal(sem, to):
        pl.semaphore_signal(sem, inc=1, device_id={AXIS: to}, device_id_type=MESH)

    def remote(source, landing, to, stream):
        return pltpu.make_async_remote_copy(
            src_ref=source,
            dst_ref=landing,
            send_sem=send_sem.at[stream],
            recv_sem=recv_sem.at[stream],
            device_id={AXIS: to},
            device_id_type=MESH,
        )

    barrier = pltpu.get_barrier_semaphore()
    for turn in range(1, rows):
        signal(barrier, (row + turn) % rows * ALONG_Z + place)

    @pl.when(place > 0)
    def _():
        signal(barrier, me - 1)

    @pl.when(place < last)
    def _():
        signal(barrier, me + 1)

    loads = [
        pltpu.make_async_copy(k_hbm, kv.at[0], in_sem.at[0]),
        pltpu.make_async_copy(v_hbm, kv.at[1], in_sem.at[1]),
        pltpu.make_async_copy(q_hbm, qd.at[0], in_sem.at[2]),
        pltpu.make_async_copy(g_hbm, qd.at[1], in_sem.at[3]),
        pltpu.make_async_copy(perm_hbm, perm_ref, in_sem.at[4]),
    ]
    for load in loads:
        load.start()

    greeted = rows - 1 + jnp.where(place > 0, 1, 0) + jnp.where(place < last, 1, 0)
    pl.semaphore_wait(barrier, greeted)

    @pl.when(place > 0)
    def _():
        signal(down_sem.at[0], me - 1)

    @pl.when(place < last)
    def _():
        signal(up_sem.at[0], me + 1)

    shift_kv = remote(kv, prev_kv, (me + 1) % count, 2)
    shift_qd = remote(qd, next_qd, (me + others) % count, 3)
    for load in loads[:2]:
        load.wait()

    @pl.when(place < last)
    def _():
        shift_kv.start()

    for load in loads[2:]:
        load.wait()

    @pl.when(place > 0)
    def _():
        shift_qd.start()

    def to_piece(source, held, to, stream):
        remote(source.at[:, rows_of(to, piece), :], held.at[me], to, stream).start()

    def to_column(there):
        for turn in range(rows):
            to_piece(kv, held_kv, (row + turn) % rows * ALONG_Z + there, 0)

    for turn in range(1, rows):
        to_piece(kv, held_kv, (row + turn) % rows * ALONG_Z + place, 0)

    def below(step, carry):
        pl.semaphore_wait(up_sem.at[step], 1)

        @pl.when(place < last)
        def _():
            signal(up_sem.at[step + 1], me + 1)

        to_column(place - 1 - step)
        return carry

    lax.fori_loop(0, place, below, 0)

    def above(step, carry):
        pl.semaphore_wait(down_sem.at[step], 1)

        @pl.when(place > 0)
        def _():
            signal(down_sem.at[step + 1], me - 1)

        to_column(place + 1 + step)
        return carry

    lax.fori_loop(0, last - place, above, 0)

    @pl.when((place == last) & (me < others))
    def _():
        shift_kv.start()

    def all_qd(step, carry):
        to_piece(qd, held_qd, target(step, me, count), 1)
        return carry

    lax.fori_loop(0, others, all_qd, 0)

    @pl.when((place == 0) & (me > 0))
    def _():
        shift_qd.start()

    def invert(block, carry):
        found = jnp.int32(0)
        for query in range(count):
            found = jnp.where(perm_ref[0, query] == block, query, found)
        inv[block] = found
        return carry

    lax.fori_loop(0, count, invert, 0)
    held_kv[me] = kv[:, rows_of(me, piece), :]
    held_qd[me] = qd[:, rows_of(me, piece), :]

    @pl.when(me == 0)
    def _():
        prev_kv[...] = jnp.zeros_like(prev_kv)

    @pl.when(me == others)
    def _():
        next_qd[...] = jnp.zeros_like(next_qd)
        next_stats[...] = jnp.zeros_like(next_stats)

    def arrange(held, arranged, index_of):
        def reorder(block, carry):
            arranged[block] = held[index_of(block)]
            return carry

        lax.fori_loop(0, count, reorder, 0)

    def deliver(arranged, landing, stream, first, end):
        def issue(step, carry):
            to = target(step, me, count)
            remote(arranged.at[to], landing.at[:, rows_of(me, piece), :], to, stream).start()
            return carry

        lax.fori_loop(first, end, issue, 0)

    query_rows = qd[0]
    grad_rows = qd[1]
    own_scores = dot_nt(kv[0], query_rows) * scale
    own_grads = dot_nt(kv[1], grad_rows)

    @pl.when(me > 0)
    def _():
        shift_kv.wait_recv()

    prev_scores = jnp.where(me > 0, dot_nt(prev_kv[0], query_rows) * scale, -1e30)
    prev_grads = dot_nt(prev_kv[1], grad_rows)
    near_top = jnp.max(jnp.maximum(own_scores, prev_scores), axis=0, keepdims=True)
    own_probs = jnp.exp(own_scores - near_top)
    prev_probs = jnp.exp(prev_scores - near_top)
    near_total = jnp.sum(own_probs + prev_probs, axis=0, keepdims=True)
    near_mass = near_top + jnp.log(near_total)
    near_delta = (
        jnp.sum(own_probs * own_grads + prev_probs * prev_grads, axis=0, keepdims=True) / near_total
    )
    for index in range(stat_rows):
        part = near_mass if index < stat_rows // 2 else near_delta
        start = index % (stat_rows // 2) * lanes
        part_stats[index] = part[:, start : start + lanes]

    for index in range(stat_rows):

        @pl.when(me != index * stride)
        def _():
            remote(part_stats.at[index], held_stats.at[me], index * stride, 6).start()

        @pl.when(me == index * stride)
        def _():
            held_stats[me] = part_stats[index]

    await_bytes(held_kv.at[pl.ds(0, others)], recv_sem.at[0])
    arrange(held_kv, sorted_kv, lambda block: perm_ref[0, block])
    deliver(sorted_kv, far_kv, 4, 0, others)
    far_kv[:, rows_of(me, piece), :] = sorted_kv[me]

    await_bytes(held_qd.at[pl.ds(0, others)], recv_sem.at[1])
    arrange(held_qd, sorted_qd, lambda block: inv[block])
    @pl.when(me % stride == 0)
    def _():
        await_bytes(held_stats.at[pl.ds(0, others)], recv_sem.at[6])
        arrange(held_stats, sorted_stats, lambda block: inv[block])

        def issue(step, carry):
            to = target(step, me, count)
            remote(sorted_stats.at[to], far_stats.at[me // stride], to, 8).start()
            return carry

        lax.fori_loop(0, others, issue, 0)
        far_stats[me // stride] = sorted_stats[me]

    deliver(sorted_qd, far_qd, 5, 0, count // 2)
    far_qd[:, rows_of(me, piece), :] = sorted_qd[me]

    await_bytes(held_kv.at[pl.ds(0, others)], recv_sem.at[4])

    far_scores = dot_nt(far_kv[0], query_rows) * scale
    far_grads = dot_nt(far_kv[1], grad_rows)
    far_top = jnp.max(far_scores, axis=0, keepdims=True)
    top = jnp.maximum(near_top, far_top)
    far_probs = jnp.exp(far_scores - top)
    near_weight = jnp.exp(near_top - top)
    total = near_total * near_weight + jnp.sum(far_probs, axis=0, keepdims=True)
    inverse_total = 1.0 / total
    near_weight = near_weight * inverse_total
    far_probs = far_probs * inverse_total
    delta = near_delta * near_total * near_weight + jnp.sum(
        far_probs * far_grads, axis=0, keepdims=True
    )
    full_stats[...] = jnp.concatenate([top + jnp.log(total), delta], axis=0)
    deliver(sorted_qd, far_qd, 5, count // 2, others)
    tell_prev = remote(full_stats, next_stats, (me + others) % count, 7)

    @pl.when(me > 0)
    def _():
        tell_prev.start()

    attended = jnp.zeros((span, width), jnp.float32)
    grad_query = jnp.zeros((span, width), jnp.float32)
    for probs, grads, pair, own in (
        (own_probs * near_weight, own_grads, kv, True),
        (prev_probs * near_weight, prev_grads, prev_kv, False),
        (far_probs, far_grads, far_kv, False),
    ):
        low = probs.astype(jnp.bfloat16)
        grad_scores = (probs * (grads - delta) * scale).astype(jnp.bfloat16)
        attended += dot_tn(low, pair[1])
        grad_query += dot_tn(grad_scores, pair[0])
        if own:
            grad_key = dot_nn(grad_scores, query_rows)
            grad_value = dot_nn(low, grad_rows)
    o_ref[...] = attended.astype(jnp.bfloat16)
    dq_ref[...] = grad_query.astype(jnp.bfloat16)

    @pl.when(me < others)
    def _():
        shift_qd.wait_recv()
        tell_prev.wait_recv()

    next_scores = dot_nt(kv[0], next_qd[0]) * scale
    next_grads = dot_nt(kv[1], next_qd[1])
    probs = jnp.exp(next_scores - next_stats[0:1])
    low = probs.astype(jnp.bfloat16)
    grad_scores = (probs * (next_grads - next_stats[1:2]) * scale).astype(jnp.bfloat16)
    grad_key += dot_nn(grad_scores, next_qd[0])
    grad_value += dot_nn(low, next_qd[1])

    await_bytes(held_qd.at[pl.ds(0, others)], recv_sem.at[5])

    @pl.when(me % stride == 0)
    def _():
        await_bytes(far_stats.at[pl.ds(0, stat_rows - 1)], recv_sem.at[8])

    @pl.when(me % stride != 0)
    def _():
        await_bytes(far_stats, recv_sem.at[8])

    half = stat_rows // 2
    mass = jnp.concatenate([far_stats[index] for index in range(half)], axis=1)
    seen = jnp.concatenate([far_stats[half + index] for index in range(half)], axis=1)
    scores = dot_nt(kv[0], far_qd[0]) * scale
    grads = dot_nt(kv[1], far_qd[1])
    top = jnp.maximum(mass, jnp.max(scores, axis=0, keepdims=True))
    probs = jnp.exp(scores - top)
    rest = jnp.exp(mass - top)
    inverse_total = 1.0 / (rest + jnp.sum(probs, axis=0, keepdims=True))
    probs = probs * inverse_total
    delta = seen * rest * inverse_total + jnp.sum(probs * grads, axis=0, keepdims=True)
    low = probs.astype(jnp.bfloat16)
    grad_scores = (probs * (grads - delta) * scale).astype(jnp.bfloat16)
    grad_key += dot_nn(grad_scores, far_qd[0])
    grad_value += dot_nn(low, far_qd[1])
    dk_ref[...] = grad_key.astype(jnp.bfloat16)
    dv_ref[...] = grad_value.astype(jnp.bfloat16)

    for stream, held in ((0, held_kv), (1, held_qd), (4, held_kv), (5, held_qd)):
        await_bytes(held.at[pl.ds(0, others)], send_sem.at[stream])

    @pl.when(me % stride == 0)
    def _():
        await_bytes(far_stats.at[pl.ds(0, stat_rows - 1)], send_sem.at[6])
        await_bytes(held_stats.at[pl.ds(0, others)], send_sem.at[8])

    @pl.when(me % stride != 0)
    def _():
        await_bytes(far_stats, send_sem.at[6])

    @pl.when(me < others)
    def _():
        shift_kv.wait_send()

    @pl.when(me > 0)
    def _():
        shift_qd.wait_send()
        tell_prev.wait_send()


def write_kernel(*refs):
    results, places, sem = refs[:4], refs[4:8], refs[8]
    copies = [
        pltpu.make_async_copy(result, place, sem.at[index])
        for index, (result, place) in enumerate(zip(results, places))
    ]
    for copy in copies:
        copy.start()
    for copy in copies:
        copy.wait()


def body(queries, keys, values, grad_out, block_perm):
    span, width = queries.shape
    count = lax.axis_size(AXIS)
    piece = span // count
    stat_rows = 2 * span // 128
    pair = pltpu.VMEM((2, span, width), jnp.bfloat16)
    pieces = pltpu.VMEM((count, 2, piece, width), jnp.bfloat16)
    in_place = pl.BlockSpec(memory_space=pltpu.HBM)
    in_vmem = pl.BlockSpec(memory_space=pltpu.VMEM)
    result = jax.ShapeDtypeStruct((span, width), jnp.bfloat16)

    def run(*refs):
        kernel(count, *refs)

    results = pl.pallas_call(
        run,
        out_shape=(pltpu.VMEM((span, width), jnp.bfloat16),) * 4,
        in_specs=[in_place] * 5,
        out_specs=(in_vmem,) * 4,
        scratch_shapes=[
            pltpu.SMEM((1, count), jnp.int32),
            pltpu.SMEM((count,), jnp.int32),
            pair, pair, pieces, pieces, pieces, pieces, pair, pair, pair, pair,
            pltpu.VMEM((2, span), jnp.float32),
            pltpu.VMEM((2, span), jnp.float32),
            pltpu.VMEM((stat_rows, 1, 128), jnp.float32),
            pltpu.VMEM((count, 1, 128), jnp.float32),
            pltpu.VMEM((count, 1, 128), jnp.float32),
            pltpu.VMEM((stat_rows, 1, 128), jnp.float32),
            pltpu.SemaphoreType.DMA((5,)),
            pltpu.SemaphoreType.DMA((9,)),
            pltpu.SemaphoreType.DMA((9,)),
            pltpu.SemaphoreType.REGULAR((ALONG_Z,)),
            pltpu.SemaphoreType.REGULAR((ALONG_Z,)),
        ],
        compiler_params=pltpu.CompilerParams(
            collective_id=0, has_side_effects=True, vmem_limit_bytes=66400000
        ),
    )(block_perm, queries, keys, values, grad_out)
    return pl.pallas_call(
        write_kernel,
        out_shape=(result,) * 4,
        in_specs=[in_vmem] * 4,
        out_specs=(in_place,) * 4,
        scratch_shapes=[pltpu.SemaphoreType.DMA((4,))],
    )(*(pltpu.with_memory_space_constraint(result, pltpu.VMEM) for result in results))


def solution(mesh):
    placed = (
        P("seq", "head"),
        P("seq", "head"),
        P("seq", "head"),
        P("seq", "head"),
        P("head", None),
    )
    return jax.shard_map(
        body,
        mesh=mesh,
        in_specs=placed,
        out_specs=(P("seq", "head"), P("seq", "head"), P("seq", "head"), P("seq", "head")),
        check_vma=False,
    )
```

time: 87.3 us -> 74.7 us (0.86)
  Pallas kernels: 82.3 us -> 73.9 us
  local copies, waits for them, and re-layouts: 4.16 us -> 0 us
    pallas_call x1 -> x2, Pallas kernels: 82.3 us -> 73.9 us  [the longest x1 73 us: body(): pl.pallas_call(run, out_shape=(pltpu.VMEM((span, width), jnp.bfloat16),)...]
    unnamed x10 -> x0, local copies, waits for them, and re-layouts: 4.16 us -> none
where the time goes in v3:
time: 74.7 us; the launch traced here: 74.5 us
  Pallas kernels  73.9 us (99%)
    pallas_call x1, Pallas kernels, body(): pl.pallas_call(run, out_shape=(pltpu.VMEM((span, width), jnp.bfloat16),)...  73 us

profile of v3, /device:TPU:6, one launch (start us, length us, event | category | flops | bytes accessed | tf_op | source)
XLA Modules:
  0.0 74.5 jit_solution(2974529971138777162)
XLA Ops:
  0.6 73.0 %shard_map.84 = (bf16[512,128]{1,0:T(8,128)(2,1)S(1)}, bf16[512,128]{1,0:T(8,128)(2,1)S(1)}, bf16[512,128]{1,0:T(8,128)(2,1)S(1)}, bf16[512,128]{1,0:T(8,128)(2,1)S(1)}) custom-call(s32[1,32]{1,0:T(1,128)} %refs_0_.1, bf16[512,128]{1,0:T(8,128)(2,1)} %refs_1_.1, bf16[512,128]{1,0:T(8,128)(2,1)} %refs_2_.1, bf16[512,128]{1,0:T(8,128)(2,1)} %refs_3_.1, ...), custom_call_target="tpu_custom_call" | custom-call | tf_op jit(solution)/shard_map/pallas_call | solution.py:392
  73.7 0.8 %shard_map.85 = (bf16[512,128]{1,0:T(8,128)(2,1)}, bf16[512,128]{1,0:T(8,128)(2,1)}, bf16[512,128]{1,0:T(8,128)(2,1)}, bf16[512,128]{1,0:T(8,128)(2,1)}) custom-call(bf16[512,128]{1,0:T(8,128)(2,1)S(1)} %get-tuple-element.8.refs_0_, bf16[512,128]{1,0:T(8,128)(2,1)S(1)} %get-tuple-element.9.refs_1_, bf16[512,128]{1,0:T(8,128)(2,1)S(1)} %get-tuple-element.10.refs_2_, ...), custom_call_target="tpu_custom_call" | custom-call | tf_op jit(solution)/shard_map/pallas_call | solution.py:417

commit v4 on v3

--- a/solution.py
+++ b/solution.py
@@ -8,6 +8,8 @@
 MESH = pl.DeviceIdType.MESH
 AXIS = "seq"
 ALONG_Z = 8
+QD_EARLY = 24
+QD_FIRST = 16
 
 
 def dot_nt(left, right):
@@ -54,6 +56,7 @@
     place = me % ALONG_Z
     row = me // ALONG_Z
     last = ALONG_Z - 1
+    half = ALONG_Z // 2
     lanes = 128
     stat_rows = 2 * span // lanes
     stride = count // stat_rows
@@ -113,13 +116,6 @@
     def _():
         shift_kv.start()
 
-    for load in loads[2:]:
-        load.wait()
-
-    @pl.when(place > 0)
-    def _():
-        shift_qd.start()
-
     def to_piece(source, held, to, stream):
         remote(source.at[:, rows_of(to, piece), :], held.at[me], to, stream).start()
 
@@ -158,15 +154,36 @@
     def _():
         shift_kv.start()
 
+    for load in loads[2:]:
+        load.wait()
+
+    own_side = place // half * half
+
+    def near_rows(index):
+        start = (index * ALONG_Z + own_side) * piece
+        return pl.ds(pl.multiple_of(start, half * piece), half * piece)
+
+    crosses = (place == half) | ((place == 0) & (me > 0))
+
+    def shift_part(index):
+        part = (slice(None), near_rows(index), slice(None))
+        return remote(qd.at[part], next_qd.at[part], (me + others) % count, 3)
+
+    @pl.when(crosses)
+    def _():
+        for index in range(rows):
+            shift_part(index).start()
+
+    @pl.when((place > 0) & (place != half))
+    def _():
+        shift_qd.start()
     def all_qd(step, carry):
         to_piece(qd, held_qd, target(step, me, count), 1)
         return carry
 
-    lax.fori_loop(0, others, all_qd, 0)
-
-    @pl.when((place == 0) & (me > 0))
-    def _():
-        shift_qd.start()
+    @pl.when(place == 0)
+    def _():
+        lax.fori_loop(0, QD_FIRST, all_qd, 0)
 
     def invert(block, carry):
         found = jnp.int32(0)
@@ -237,6 +254,8 @@
         def _():
             held_stats[me] = part_stats[index]
 
+    lax.fori_loop(jnp.where(place == 0, QD_FIRST, 0), others, all_qd, 0)
+
     await_bytes(held_kv.at[pl.ds(0, others)], recv_sem.at[0])
     arrange(held_kv, sorted_kv, lambda block: perm_ref[0, block])
     deliver(sorted_kv, far_kv, 4, 0, others)
@@ -257,7 +276,32 @@
         lax.fori_loop(0, others, issue, 0)
         far_stats[me // stride] = sorted_stats[me]
 
-    deliver(sorted_qd, far_qd, 5, 0, count // 2)
+    def forward(index):
+        there = index * ALONG_Z + jnp.where(place < half, half - 1, last)
+        origin = there + 1
+        part = (slice(None), rows_of(me, piece), slice(None))
+        meant = (origin < count) & (there != me)
+        return meant, pltpu.make_async_remote_copy(
+            src_ref=held_qd.at[origin % count],
+            dst_ref=next_qd.at[part],
+            send_sem=send_sem.at[9],
+            recv_sem=recv_sem.at[3],
+            device_id={AXIS: there},
+            device_id_type=MESH,
+        )
+
+    for index in range(rows):
+        meant, copy = forward(index)
+
+        @pl.when(meant)
+        def _():
+            copy.start()
+
+    @pl.when(((place == half - 1) | (place == last)) & (me < others))
+    def _():
+        next_qd[:, rows_of(me, piece), :] = held_qd[(me + 1) % count]
+
+    deliver(sorted_qd, far_qd, 5, 0, QD_EARLY)
     far_qd[:, rows_of(me, piece), :] = sorted_qd[me]
 
     await_bytes(held_kv.at[pl.ds(0, others)], recv_sem.at[4])
@@ -276,7 +320,7 @@
         far_probs * far_grads, axis=0, keepdims=True
     )
     full_stats[...] = jnp.concatenate([top + jnp.log(total), delta], axis=0)
-    deliver(sorted_qd, far_qd, 5, count // 2, others)
+    deliver(sorted_qd, far_qd, 5, QD_EARLY, others)
     tell_prev = remote(full_stats, next_stats, (me + others) % count, 7)
 
     @pl.when(me > 0)
@@ -300,9 +344,17 @@
     o_ref[...] = attended.astype(jnp.bfloat16)
     dq_ref[...] = grad_query.astype(jnp.bfloat16)
 
+    gathers = ((place == half - 1) | (place == last)) & (me < others)
+
+    @pl.when(gathers)
+    def _():
+        await_bytes(next_qd.at[:, pl.ds(0, span - piece), :], recv_sem.at[3])
+
+    @pl.when((place != half - 1) & (place != last))
+    def _():
+        shift_qd.wait_recv()
     @pl.when(me < others)
     def _():
-        shift_qd.wait_recv()
         tell_prev.wait_recv()
 
     next_scores = dot_nt(kv[0], next_qd[0]) * scale
@@ -323,9 +375,9 @@
     def _():
         await_bytes(far_stats, recv_sem.at[8])
 
-    half = stat_rows // 2
-    mass = jnp.concatenate([far_stats[index] for index in range(half)], axis=1)
-    seen = jnp.concatenate([far_stats[half + index] for index in range(half)], axis=1)
+    stat_half = stat_rows // 2
+    mass = jnp.concatenate([far_stats[index] for index in range(stat_half)], axis=1)
+    seen = jnp.concatenate([far_stats[stat_half + index] for index in range(stat_half)], axis=1)
     scores = dot_nt(kv[0], far_qd[0]) * scale
     grads = dot_nt(kv[1], far_qd[1])
     top = jnp.maximum(mass, jnp.max(scores, axis=0, keepdims=True))
@@ -357,9 +409,23 @@
     def _():
         shift_kv.wait_send()
 
+
+    @pl.when(crosses)
+    def _():
+        await_bytes(next_qd.at[:, pl.ds(0, span // 2), :], send_sem.at[3])
+
+    @pl.when((place > 0) & (place != half))
+    def _():
+        shift_qd.wait_send()
+
+    for index in range(rows):
+        meant, copy = forward(index)
+
+        @pl.when(meant)
+        def _():
+            copy.wait_send()
     @pl.when(me > 0)
     def _():
-        shift_qd.wait_send()
         tell_prev.wait_send()
 
 
@@ -405,7 +471,7 @@
             pltpu.VMEM((count, 1, 128), jnp.float32),
             pltpu.VMEM((stat_rows, 1, 128), jnp.float32),
             pltpu.SemaphoreType.DMA((5,)),
-            pltpu.SemaphoreType.DMA((9,)),
+            pltpu.SemaphoreType.DMA((10,)),
             pltpu.SemaphoreType.DMA((9,)),
             pltpu.SemaphoreType.REGULAR((ALONG_Z,)),
             pltpu.SemaphoreType.REGULAR((ALONG_Z,)),

time: 74.7 us -> 70.6 us (0.945)
  Pallas kernels: 73.9 us -> 69.8 us
    pallas_call x1, Pallas kernels: 73 us -> 69 us  [body(): pl.pallas_call(run, out_shape=(pltpu.VMEM((span, width), jnp.bfloat16),)...]
where the time goes in v4:
time: 70.6 us; the launch traced here: 70.4 us
  Pallas kernels  69.8 us (99%)
    pallas_call x1, Pallas kernels, body(): pl.pallas_call(run, out_shape=(pltpu.VMEM((span, width), jnp.bfloat16),)...  69 us

profile of v4, /device:TPU:6, one launch (start us, length us, event | category | flops | bytes accessed | tf_op | source)
XLA Modules:
  0.0 70.4 jit_solution(7365169716763422742)
XLA Ops:
  0.6 69.0 %shard_map.84 = (bf16[512,128]{1,0:T(8,128)(2,1)S(1)}, bf16[512,128]{1,0:T(8,128)(2,1)S(1)}, bf16[512,128]{1,0:T(8,128)(2,1)S(1)}, bf16[512,128]{1,0:T(8,128)(2,1)S(1)}) custom-call(s32[1,32]{1,0:T(1,128)} %refs_0_.1, bf16[512,128]{1,0:T(8,128)(2,1)} %refs_1_.1, bf16[512,128]{1,0:T(8,128)(2,1)} %refs_2_.1, bf16[512,128]{1,0:T(8,128)(2,1)} %refs_3_.1, ...), custom_call_target="tpu_custom_call" | custom-call | tf_op jit(solution)/shard_map/pallas_call | solution.py:458
  69.6 0.8 %shard_map.85 = (bf16[512,128]{1,0:T(8,128)(2,1)}, bf16[512,128]{1,0:T(8,128)(2,1)}, bf16[512,128]{1,0:T(8,128)(2,1)}, bf16[512,128]{1,0:T(8,128)(2,1)}) custom-call(bf16[512,128]{1,0:T(8,128)(2,1)S(1)} %get-tuple-element.8.refs_0_, bf16[512,128]{1,0:T(8,128)(2,1)S(1)} %get-tuple-element.9.refs_1_, bf16[512,128]{1,0:T(8,128)(2,1)S(1)} %get-tuple-element.10.refs_2_, ...), custom_call_target="tpu_custom_call" | custom-call | tf_op jit(solution)/shard_map/pallas_call | solution.py:483

commit v5 on v4

--- a/solution.py
+++ b/solution.py
@@ -29,6 +29,14 @@
     turn = (step + 1) % (count // ALONG_Z)
     along = (ALONG_Z // 2 + (1 - 2 * (ring % 2)) * ((ring + 1) // 2)) % ALONG_Z
     place = (me % ALONG_Z + along) % ALONG_Z
+    row = (me // ALONG_Z + turn) % (count // ALONG_Z)
+    return row * ALONG_Z + place
+
+
+def outward(step, me, count):
+    ring = step // (count // ALONG_Z)
+    turn = step % (count // ALONG_Z)
+    place = (ring % 2) * (ALONG_Z - 1) + (1 - 2 * (ring % 2)) * (ring // 2)
     row = (me // ALONG_Z + turn) % (count // ALONG_Z)
     return row * ALONG_Z + place
 
@@ -169,14 +177,6 @@
         part = (slice(None), near_rows(index), slice(None))
         return remote(qd.at[part], next_qd.at[part], (me + others) % count, 3)
 
-    @pl.when(crosses)
-    def _():
-        for index in range(rows):
-            shift_part(index).start()
-
-    @pl.when((place > 0) & (place != half))
-    def _():
-        shift_qd.start()
     def all_qd(step, carry):
         to_piece(qd, held_qd, target(step, me, count), 1)
         return carry
@@ -214,8 +214,12 @@
 
     def deliver(arranged, landing, stream, first, end):
         def issue(step, carry):
-            to = target(step, me, count)
-            remote(arranged.at[to], landing.at[:, rows_of(me, piece), :], to, stream).start()
+            to = outward(step, me, count)
+
+            @pl.when(to != me)
+            def _():
+                remote(arranged.at[to], landing.at[:, rows_of(me, piece), :], to, stream).start()
+
             return carry
 
         lax.fori_loop(first, end, issue, 0)
@@ -258,9 +262,17 @@
 
     await_bytes(held_kv.at[pl.ds(0, others)], recv_sem.at[0])
     arrange(held_kv, sorted_kv, lambda block: perm_ref[0, block])
-    deliver(sorted_kv, far_kv, 4, 0, others)
+    deliver(sorted_kv, far_kv, 4, 0, count)
     far_kv[:, rows_of(me, piece), :] = sorted_kv[me]
 
+    @pl.when(crosses)
+    def _():
+        for index in range(rows):
+            shift_part(index).start()
+
+    @pl.when((place > 0) & (place != half))
+    def _():
+        shift_qd.start()
     await_bytes(held_qd.at[pl.ds(0, others)], recv_sem.at[1])
     arrange(held_qd, sorted_qd, lambda block: inv[block])
     @pl.when(me % stride == 0)
@@ -320,7 +332,7 @@
         far_probs * far_grads, axis=0, keepdims=True
     )
     full_stats[...] = jnp.concatenate([top + jnp.log(total), delta], axis=0)
-    deliver(sorted_qd, far_qd, 5, QD_EARLY, others)
+    deliver(sorted_qd, far_qd, 5, QD_EARLY, count)
     tell_prev = remote(full_stats, next_stats, (me + others) % count, 7)
 
     @pl.when(me > 0)

time: 70.6 us -> 69.2 us (0.980)
  Pallas kernels: 69.8 us -> 68 us
    pallas_call x1, Pallas kernels: 69 us -> 67.1 us  [body(): pl.pallas_call(run, out_shape=(pltpu.VMEM((span, width), jnp.bfloat16),)...]
where the time goes in v5:
time: 69.2 us; the launch traced here: 68.6 us
  Pallas kernels  68 us (98%)
    pallas_call x1, Pallas kernels, body(): pl.pallas_call(run, out_shape=(pltpu.VMEM((span, width), jnp.bfloat16),)...  67.1 us

profile of v5, /device:TPU:6, one launch (start us, length us, event | category | flops | bytes accessed | tf_op | source)
XLA Modules:
  0.0 68.6 jit_solution(11015387708401681236)
XLA Ops:
  0.6 67.1 %shard_map.84 = (bf16[512,128]{1,0:T(8,128)(2,1)S(1)}, bf16[512,128]{1,0:T(8,128)(2,1)S(1)}, bf16[512,128]{1,0:T(8,128)(2,1)S(1)}, bf16[512,128]{1,0:T(8,128)(2,1)S(1)}) custom-call(s32[1,32]{1,0:T(1,128)} %refs_0_.1, bf16[512,128]{1,0:T(8,128)(2,1)} %refs_1_.1, bf16[512,128]{1,0:T(8,128)(2,1)} %refs_2_.1, bf16[512,128]{1,0:T(8,128)(2,1)} %refs_3_.1, ...), custom_call_target="tpu_custom_call" | custom-call | tf_op jit(solution)/shard_map/pallas_call | solution.py:470
  67.8 0.8 %shard_map.85 = (bf16[512,128]{1,0:T(8,128)(2,1)}, bf16[512,128]{1,0:T(8,128)(2,1)}, bf16[512,128]{1,0:T(8,128)(2,1)}, bf16[512,128]{1,0:T(8,128)(2,1)}) custom-call(bf16[512,128]{1,0:T(8,128)(2,1)S(1)} %get-tuple-element.8.refs_0_, bf16[512,128]{1,0:T(8,128)(2,1)S(1)} %get-tuple-element.9.refs_1_, bf16[512,128]{1,0:T(8,128)(2,1)S(1)} %get-tuple-element.10.refs_2_, ...), custom_call_target="tpu_custom_call" | custom-call | tf_op jit(solution)/shard_map/pallas_call | solution.py:495

commit v6 on v5

--- a/solution.py
+++ b/solution.py
@@ -37,8 +37,7 @@
     ring = step // (count // ALONG_Z)
     turn = step % (count // ALONG_Z)
     place = (ring % 2) * (ALONG_Z - 1) + (1 - 2 * (ring % 2)) * (ring // 2)
-    row = (me // ALONG_Z + turn) % (count // ALONG_Z)
-    return row * ALONG_Z + place
+    return turn * ALONG_Z + place
 
 
 def rows_of(index, size):

time: 69.2 us -> 68.8 us (level)
  Pallas kernels: 68 us -> 66.9 us
    pallas_call x1, Pallas kernels: 67.1 us -> 66.1 us  [body(): pl.pallas_call(run, out_shape=(pltpu.VMEM((span, width), jnp.bfloat16),)...]
where the time goes in v6:
time: 68.8 us; the launch traced here: 67.6 us
  Pallas kernels  66.9 us (97%)
    pallas_call x1, Pallas kernels, body(): pl.pallas_call(run, out_shape=(pltpu.VMEM((span, width), jnp.bfloat16),)...  66.1 us

profile of v6, /device:TPU:6, one launch (start us, length us, event | category | flops | bytes accessed | tf_op | source)
XLA Modules:
  0.0 67.6 jit_solution(14157916762215405224)
XLA Ops:
  0.6 66.1 %shard_map.84 = (bf16[512,128]{1,0:T(8,128)(2,1)S(1)}, bf16[512,128]{1,0:T(8,128)(2,1)S(1)}, bf16[512,128]{1,0:T(8,128)(2,1)S(1)}, bf16[512,128]{1,0:T(8,128)(2,1)S(1)}) custom-call(s32[1,32]{1,0:T(1,128)} %refs_0_.1, bf16[512,128]{1,0:T(8,128)(2,1)} %refs_1_.1, bf16[512,128]{1,0:T(8,128)(2,1)} %refs_2_.1, bf16[512,128]{1,0:T(8,128)(2,1)} %refs_3_.1, ...), custom_call_target="tpu_custom_call" | custom-call | tf_op jit(solution)/shard_map/pallas_call | solution.py:469
  66.8 0.8 %shard_map.85 = (bf16[512,128]{1,0:T(8,128)(2,1)}, bf16[512,128]{1,0:T(8,128)(2,1)}, bf16[512,128]{1,0:T(8,128)(2,1)}, bf16[512,128]{1,0:T(8,128)(2,1)}) custom-call(bf16[512,128]{1,0:T(8,128)(2,1)S(1)} %get-tuple-element.8.refs_0_, bf16[512,128]{1,0:T(8,128)(2,1)S(1)} %get-tuple-element.9.refs_1_, bf16[512,128]{1,0:T(8,128)(2,1)S(1)} %get-tuple-element.10.refs_2_, ...), custom_call_target="tpu_custom_call" | custom-call | tf_op jit(solution)/shard_map/pallas_call | solution.py:494
